TPU v7x, 512 devices: a whole 4x4x16 slice. The times are simulated.
512 devices in a mesh: doc: 16 (over y_hi, x, core), seq: 32 (over z, y_lo).
Axes of the slice: x: 4, y: 4 (y_hi: 2, y_lo: 2; y = y_hi * 2 + y_lo), z: 16, core: 2. Of those that a mesh axis runs over, the one named last changes fastest.
Arguments:
- queries: bfloat16 [16, 4096, 1024], P('doc', 'seq'), may hold values from -7 to 7
- key_rows: bfloat16 [16, 4096, 1024], P('doc', 'seq'), may hold values from -7 to 7
- value_rows: bfloat16 [16, 4096, 1024], P('doc', 'seq'), may hold values from -5 to 5
- cotangent: bfloat16 [16, 4096, 1024], P('doc', 'seq'), may hold values from -3 to 3
- out_weight: bfloat16 [1024, 1024], P('doc'), may hold values from -0.1875 to 0.1875
- lengths: int32 [16, 4], P('doc'), may hold values from 1 to 32, 64 in all within a row
- upweight: int32 [16, 4], P('doc'), may hold values from 1 to 6, as said below
Outputs:
- layer_out: bfloat16 [16, 4096, 1024], P('doc', 'seq')
- grad_query: bfloat16 [16, 4096, 1024], P('doc', 'seq')
- grad_key: bfloat16 [16, 4096, 1024], P('doc', 'seq')
- grad_value: bfloat16 [16, 4096, 1024], P('doc', 'seq')
- grad_weight: float32 [1024, 1024], P('doc')
Inputs may be any that keep to these rules, and one draw needn't show every extreme that they name: Each sequence's documents fill it exactly: the lengths add up to 64, and the longest is 32. `upweight`: each entry is 1 or 6; every sequence has a document with factor 6.
All inputs are finite; a program needn't handle non-finite values.
Results may differ from a plain program's by a relative error of at most 0.0089.
Values may be sent and summed in bfloat16 or wider, within the bound.
A program may use at most 128 MiB of HBM per device.

v0:
```python
import math

import jax
import jax.numpy as jnp
from jax import lax
from jax.sharding import PartitionSpec as P

HEADS = 16
HEAD_DIM = 64
WINDOW = 512
BLOCK = 64
DOCS = 4


def shifted(value, axis, steps):
    count = lax.axis_size(axis)
    first, last = (max(0, -steps), min(count, count - steps))
    return lax.ppermute(value, axis, [(source, source + steps) for source in range(first, last)])


def document_ids(lengths_row, positions):
    bounds = jnp.cumsum(lengths_row) * BLOCK
    return jnp.sum((positions[:, None] >= bounds[None, :]).astype(jnp.int32), axis=1)


def band_mask(query_pos, key_pos, query_doc, key_doc, seq_len):
    near_band = jnp.abs(query_pos[:, None] - key_pos[None, :]) <= WINDOW
    inside = (key_pos >= 0) & (key_pos < seq_len)
    return near_band & inside[None, :] & (query_doc[:, None] == key_doc[None, :])


def soft_weights(query_grp, key_grp, allowed):
    scores = jnp.einsum(
        "qhd,khd->hqk", query_grp, key_grp, preferred_element_type=jnp.float32
    ) * HEAD_DIM ** (-0.5)
    scores = jnp.where(allowed[None], scores, -jnp.inf)
    row_peak = jnp.max(scores, axis=2, keepdims=True)
    exponent = jnp.exp(scores - row_peak)
    return exponent / jnp.sum(exponent, axis=2, keepdims=True)


def body(queries, key_rows, value_rows, cotangent, out_weight, lengths, upweight):
    rows_here = queries.shape[1]
    model_width = queries.shape[2]
    seq_count = lax.axis_size("seq")
    doc_count = lax.axis_size("doc")
    seq_place = lax.axis_index("seq")
    seq_len = rows_here * seq_count
    edge_rows = min(WINDOW, rows_here)
    far_blocks = WINDOW // edge_rows
    key_span = rows_here + 2 * WINDOW
    score_scale = HEAD_DIM ** (-0.5)
    query_rows = queries[0]
    stacked = jnp.stack([key_rows[0], value_rows[0]])
    before_list = [shifted(stacked, "seq", distance) for distance in range(1, far_blocks + 1)]
    after_list = [shifted(stacked, "seq", -distance) for distance in range(1, far_blocks + 1)]
    extended = jnp.concatenate(before_list[::-1] + [stacked] + after_list, axis=1)
    key_ext = extended[0]
    value_ext = extended[1]
    row_base = seq_place * rows_here
    query_pos = row_base + jnp.arange(rows_here, dtype=jnp.int32)
    key_pos = row_base - WINDOW + jnp.arange(key_span, dtype=jnp.int32)
    lengths_row = lengths[0]
    query_doc = document_ids(lengths_row, query_pos)
    allowed = band_mask(query_pos, key_pos, query_doc, document_ids(lengths_row, key_pos), seq_len)
    matches = query_doc[:, None] == jnp.arange(DOCS, dtype=jnp.int32)[None, :]
    token_weight = jnp.sum(jnp.where(matches, upweight[0][None, :], 0), axis=1).astype(jnp.float32)
    group_heads = min(HEADS, max(1, 512 // rows_here))
    group_count = HEADS // group_heads
    group_cols = group_heads * HEAD_DIM

    def group_slices(group_index):
        col_start = group_index * group_cols
        query_grp = lax.dynamic_slice_in_dim(query_rows, col_start, group_cols, 1).reshape(
            rows_here, group_heads, HEAD_DIM
        )
        key_grp = lax.dynamic_slice_in_dim(key_ext, col_start, group_cols, 1).reshape(
            key_span, group_heads, HEAD_DIM
        )
        value_grp = lax.dynamic_slice_in_dim(value_ext, col_start, group_cols, 1).reshape(
            key_span, group_heads, HEAD_DIM
        )
        return (col_start, query_grp, key_grp, value_grp)

    def forward_group(group_index, attended_buf):
        col_start, query_grp, key_grp, value_grp = group_slices(group_index)
        prob_half = soft_weights(query_grp, key_grp, allowed).astype(jnp.bfloat16)
        mixed_rows = jnp.einsum(
            "hqk,khd->qhd", prob_half, value_grp, preferred_element_type=jnp.float32
        )
        mixed_rows = mixed_rows.reshape(rows_here, group_cols).astype(jnp.bfloat16)
        return lax.dynamic_update_slice_in_dim(attended_buf, mixed_rows, col_start, 1)

    attended = lax.fori_loop(
        0, group_count, forward_group, jnp.zeros((rows_here, model_width), jnp.bfloat16)
    )
    full_weight = lax.all_gather(out_weight, "doc", axis=0, tiled=True)
    layer_out = jnp.dot(attended, full_weight, preferred_element_type=jnp.float32).astype(
        jnp.bfloat16
    )
    grad_out = (token_weight[:, None] * cotangent[0].astype(jnp.float32)).astype(jnp.bfloat16)
    grad_attended = lax.dot_general(
        grad_out, full_weight, (((1,), (1,)), ((), ())), preferred_element_type=jnp.float32
    ).astype(jnp.bfloat16)
    partial_grad = lax.dot_general(
        attended, grad_out, (((0,), (0,)), ((), ())), preferred_element_type=jnp.float32
    )
    row_block = lax.psum_scatter(partial_grad, "doc", scatter_dimension=0, tiled=True)
    weight_sum = lax.psum(row_block, "seq")
    grad_weight = weight_sum * (1.0 / math.sqrt(rows_here * seq_count * doc_count))

    def backward_group(group_index, grad_state):
        grad_query_buf, own_grad, early_grad, later_grad = grad_state
        col_start, query_grp, key_grp, value_grp = group_slices(group_index)
        prob_full = soft_weights(query_grp, key_grp, allowed)
        prob_half = prob_full.astype(jnp.bfloat16)
        grad_grp = lax.dynamic_slice_in_dim(grad_attended, col_start, group_cols, 1).reshape(
            rows_here, group_heads, HEAD_DIM
        )
        grad_prob = jnp.einsum(
            "qhd,khd->hqk", grad_grp, value_grp, preferred_element_type=jnp.float32
        )
        centre = jnp.sum(prob_full * grad_prob, axis=2, keepdims=True)
        grad_score = (prob_full * (grad_prob - centre) * score_scale).astype(jnp.bfloat16)
        grad_query_grp = jnp.einsum(
            "hqk,khd->qhd", grad_score, key_grp, preferred_element_type=jnp.float32
        )
        grad_query_grp = grad_query_grp.reshape(rows_here, group_cols).astype(jnp.bfloat16)
        key_part = jnp.einsum(
            "hqk,qhd->khd", grad_score, query_grp, preferred_element_type=jnp.float32
        )
        value_part = jnp.einsum(
            "hqk,qhd->khd", prob_half, grad_grp, preferred_element_type=jnp.float32
        )
        both_parts = jnp.stack(
            [key_part.reshape(key_span, group_cols), value_part.reshape(key_span, group_cols)]
        )
        grad_query_buf = lax.dynamic_update_slice_in_dim(
            grad_query_buf, grad_query_grp, col_start, 1
        )
        own_grad = lax.dynamic_update_slice(
            own_grad, both_parts[:, WINDOW : WINDOW + rows_here], (0, 0, col_start)
        )
        early_grad = lax.dynamic_update_slice(
            early_grad, both_parts[:, :WINDOW].astype(jnp.bfloat16), (0, 0, col_start)
        )
        later_grad = lax.dynamic_update_slice(
            later_grad, both_parts[:, WINDOW + rows_here :].astype(jnp.bfloat16), (0, 0, col_start)
        )
        return (grad_query_buf, own_grad, early_grad, later_grad)

    grad_state = (
        jnp.zeros((rows_here, model_width), jnp.bfloat16),
        jnp.zeros((2, rows_here, model_width), jnp.float32),
        jnp.zeros((2, WINDOW, model_width), jnp.bfloat16),
        jnp.zeros((2, WINDOW, model_width), jnp.bfloat16),
    )
    grad_query, own_grad, early_grad, later_grad = lax.fori_loop(
        0, group_count, backward_group, grad_state
    )
    early_returned = [
        shifted(
            early_grad[:, WINDOW - distance * edge_rows : WINDOW - (distance - 1) * edge_rows],
            "seq",
            -distance,
        )
        for distance in range(1, far_blocks + 1)
    ]
    later_returned = [
        shifted(later_grad[:, (distance - 1) * edge_rows : distance * edge_rows], "seq", distance)
        for distance in range(1, far_blocks + 1)
    ]
    tail_extra = jnp.zeros((2, edge_rows, model_width), jnp.float32)
    for returned in early_returned:
        tail_extra = tail_extra + returned.astype(jnp.float32)
    head_extra = jnp.zeros((2, edge_rows, model_width), jnp.float32)
    for returned in later_returned:
        head_extra = head_extra + returned.astype(jnp.float32)
    own_grad = own_grad.at[:, rows_here - edge_rows :].add(tail_extra)
    own_grad = own_grad.at[:, :edge_rows].add(head_extra)
    grad_key = own_grad[0].astype(jnp.bfloat16)
    grad_value = own_grad[1].astype(jnp.bfloat16)
    return (layer_out[None], grad_query[None], grad_key[None], grad_value[None], grad_weight)


def solution(mesh):
    return jax.shard_map(
        body,
        mesh=mesh,
        in_specs=(
            P("doc", "seq", None),
            P("doc", "seq", None),
            P("doc", "seq", None),
            P("doc", "seq", None),
            P("doc", None),
            P("doc", None),
            P("doc", None),
        ),
        out_specs=(
            P("doc", "seq", None),
            P("doc", "seq", None),
            P("doc", "seq", None),
            P("doc", "seq", None),
            P("doc", None),
        ),
        check_vma=False,
    )
```

profile of v0, /device:TPU:6, one launch (start us, length us, event | category | flops | bytes accessed | tf_op | source)
XLA Modules:
  0.0 587.7 jit_solution(5047850334984720192)
XLA Ops:
  9.6 6.0 %collective-permute-start = (bf16[2,128,1024]{1,2,0:T(8,128)(2,1)S(1)}, bf16[2,128,1024]{1,2,0:T(8,128)(2,1)}, u32[]{:S(2)}, u32[]{:S(2)}) collective-permute-start(bf16[2,128,1024]{1,2,0:T(8,128)(2,1)S(1)} %pad_maximum_fusion.1), channel_id=1, source_target_pairs={{0,4},{1,5},{2,6},{3,7},{4,8},{5,9},{6,10},{7,11},{8,12},{9,13},{1... | collective-permute-start | bytes 1572872 | tf_op jit(solution)/shard_map/ppermute | solution.py:18
  15.5 4.9 collective-permute-start.1
  20.4 4.3 collective-permute-start.2
  24.7 3.7 collective-permute-start.3
  34.9 6.6 %collective-permute-done.1 = bf16[2,128,1024]{1,2,0:T(8,128)(2,1)S(1)} collective-permute-done((bf16[2,128,1024]{1,2,0:T(8,128)(2,1)S(1)}, bf16[2,128,1024]{1,2,0:T(8,128)(2,1)S(1)}, u32[]{:S(2)}, u32[]{:S(2)}) %collective-permute-start.1) | collective-permute-done | bytes 524320 | tf_op jit(solution)/shard_map/ppermute | solution.py:18
  42.9 8.7 %collective-permute-done.2 = bf16[2,128,1024]{1,2,0:T(8,128)(2,1)S(1)} collective-permute-done((bf16[2,128,1024]{1,2,0:T(8,128)(2,1)S(1)}, bf16[2,128,1024]{1,2,0:T(8,128)(2,1)S(1)}, u32[]{:S(2)}, u32[]{:S(2)}) %collective-permute-start.2) | collective-permute-done | bytes 524320 | tf_op jit(solution)/shard_map/ppermute | solution.py:18
  55.2 21.0 %collective-permute-done.6 = bf16[2,128,1024]{1,2,0:T(8,128)(2,1)S(1)} collective-permute-done((bf16[2,128,1024]{1,2,0:T(8,128)(2,1)S(1)}, bf16[2,128,1024]{1,2,0:T(8,128)(2,1)S(1)}, u32[]{:S(2)}, u32[]{:S(2)}) %collective-permute-start.6) | collective-permute-done | bytes 524320 | tf_op jit(solution)/shard_map/ppermute | solution.py:18
  76.3 30.6 %collective-permute-done.7 = bf16[2,128,1024]{1,2,0:T(8,128)(2,1)S(1)} collective-permute-done((bf16[2,128,1024]{1,2,0:T(8,128)(2,1)S(1)}, bf16[2,128,1024]{1,2,0:T(8,128)(2,1)S(1)}, u32[]{:S(2)}, u32[]{:S(2)}) %collective-permute-start.7) | collective-permute-done | bytes 524320 | tf_op jit(solution)/shard_map/ppermute | solution.py:18
  107.0 2.5 slice_bitcast_fusion
  109.6 29.0 %while.38 = (s32[]{:T(128)}, bf16[128,1024]{0,1:T(8,128)(2,1)S(1)}, bf16[1152,1024]{0,1:T(8,128)(2,1)}, bf16[128,1024]{0,1:T(8,128)(2,1)}, bf16[1152,1024]{0,1:T...) while((s32[]{:T(128)}, bf16[128,1024]{0,1:T(8,128)(2,1)S(1)}, ...), condition=%wide.region_6.7_spmd.clone, body=%wide.region_3.6_spmd.clone.sunk | while | flops 155452544 | bytes 8961351 | solution.py:94
  138.6 2.7 fusion.51
  141.6 3.1 convolution_convert_fusion
  149.8 94.7 %while.39 = (s32[]{:T(128)}, bf16[128,1024]{1,0:T(8,128)(2,1)}, f32[2,128,1024]{2,1,0:T(8,128)}, bf16[2,512,1024]{2,1,0:T(8,128)(2,1)}, bf16[2,512,1024]{2,1,0:T...) while((s32[]{:T(128)}, bf16[128,1024]{1,0:T(8,128)(2,1)}, ...), condition=%wide.region_12.13_spmd.clone, body=%wide.region_8.12_spmd.clone.sunk | while | flops 390861184 | bytes 38351472 | solution.py:158
  157.8 4.7 fusion.119
  163.4 5.2 fusion.120
  179.4 2.4 fusion.118
  181.8 4.7 fusion.119
  187.3 5.0 fusion.120
  203.0 2.4 fusion.118
  205.4 4.7 fusion.119
  210.9 5.0 fusion.120
  228.9 4.7 fusion.119
  234.4 5.2 fusion.120
  244.6 2.7 fusion.58
  247.3 11.6 %collective-permute-start.15 = (bf16[2,128,1024]{2,1,0:T(8,128)(2,1)S(1)}, bf16[2,128,1024]{2,1,0:T(8,128)(2,1)S(1)}, u32[]{:S(2)}, u32[]{:S(2)}) collective-permute-start(bf16[2,128,1024]{2,1,0:T(8,128)(2,1)S(1)} %get-tuple-element.488), channel_id=1, source_target_pairs={{0,4},{1,5},{2,6},{3,7},{4,8},{5,9},{6,10},{7,11},{8,12},{9,13},{1... | collective-permute-start | bytes 1572872 | tf_op jit(solution)/shard_map/ppermute | solution.py:18
  261.6 6.1 %collective-permute-start.12 = (bf16[2,128,1024]{2,1,0:T(8,128)(2,1)}, bf16[2,128,1024]{2,1,0:T(8,128)(2,1)S(1)}, u32[]{:S(2)}, u32[]{:S(2)}) collective-permute-start(bf16[2,128,1024]{2,1,0:T(8,128)(2,1)} %get-tuple-element.485), channel_id=1, source_target_pairs={{0,1},{1,2},{2,3},{3,4},{4,5},{5,6},{6,7},{7,8},{8,9},{9,10},{10,1... | collective-permute-start | bytes 1572872 | tf_op jit(solution)/shard_map/ppermute | solution.py:18
  272.5 10.0 %collective-permute-done.14 = bf16[2,128,1024]{2,1,0:T(8,128)(2,1)S(1)} collective-permute-done((bf16[2,128,1024]{2,1,0:T(8,128)(2,1)S(1)}, bf16[2,128,1024]{2,1,0:T(8,128)(2,1)S(1)}, u32[]{:S(2)}, u32[]{:S(2)}) %collective-permute-start.14) | collective-permute-done | bytes 524320 | tf_op jit(solution)/shard_map/ppermute | solution.py:18
  283.8 8.5 %collective-permute-done.13 = bf16[2,128,1024]{2,1,0:T(8,128)(2,1)S(1)} collective-permute-done((bf16[2,128,1024]{2,1,0:T(8,128)(2,1)S(1)}, bf16[2,128,1024]{2,1,0:T(8,128)(2,1)S(1)}, u32[]{:S(2)}, u32[]{:S(2)}) %collective-permute-start.13) | collective-permute-done | bytes 524320 | tf_op jit(solution)/shard_map/ppermute | solution.py:18
  294.8 6.7 %collective-permute-done.10 = bf16[2,128,1024]{2,1,0:T(8,128)(2,1)} collective-permute-done((bf16[2,128,1024]{2,1,0:T(8,128)(2,1)}, bf16[2,128,1024]{2,1,0:T(8,128)(2,1)}, u32[]{:S(2)}, u32[]{:S(2)}) %collective-permute-start.10) | collective-permute-done | bytes 524320 | tf_op jit(solution)/shard_map/ppermute | solution.py:18
  301.5 10.4 %collective-permute-done.9 = bf16[2,128,1024]{2,1,0:T(8,128)(2,1)} collective-permute-done((bf16[2,128,1024]{2,1,0:T(8,128)(2,1)}, bf16[2,128,1024]{2,1,0:T(8,128)(2,1)}, u32[]{:S(2)}, u32[]{:S(2)}) %collective-permute-start.9) | collective-permute-done | bytes 524320 | tf_op jit(solution)/shard_map/ppermute | solution.py:18
  312.5 2.4 add_convert_fusion
  315.8 263.7 %all-reduce.2.cloned.1.call-done = f32[64,1024]{1,0:T(8,128)} async-done(((f32[64,1024]{1,0:T(8,128)}), f32[64,1024]{1,0:T(8,128)}) %all-reduce.2.cloned.1.call-update) | async-done | bytes 262160 | tf_op jit(solution)/shard_map/psum | solution.py:109
  (241 shorter events, 112.2 us)
Async XLA Ops:
  7.2 24.3 %copy-start.8 = (bf16[1,128,1024]{2,1,0:T(8,128)(2,1)S(1)}, bf16[1,128,1024]{2,1,0:T(8,128)(2,1)}, u32[]{:S(2)}) copy-start(bf16[1,128,1024]{2,1,0:T(8,128)(2,1)} %param.19) | copy-start | bytes 786436
  7.2 134.5 %all-gather.2.cloned.1.call-start = ((), (), s32[]{:S(2)}) async-start(), calls=%async_computation.1 | async-start | bytes 2228224 | tf_op jit(solution)/shard_map/all_gather | solution.py:97
  9.6 22.9 %collective-permute-start = (bf16[2,128,1024]{1,2,0:T(8,128)(2,1)S(1)}, bf16[2,128,1024]{1,2,0:T(8,128)(2,1)}, u32[]{:S(2)}, u32[]{:S(2)}) collective-permute-start(bf16[2,128,1024]{1,2,0:T(8,128)(2,1)S(1)} %pad_maximum_fusion.1), channel_id=1, source_target_pairs={{0,4},{1,5},{2,6},{3,7},{4,8},{5,9},{6,10},{7,11},{8,12},{9,13},{1... | collective-permute-start | bytes 1572872 | tf_op jit(solution)/shard_map/ppermute | solution.py:18
  15.5 26.0 %collective-permute-start.1 = (bf16[2,128,1024]{1,2,0:T(8,128)(2,1)S(1)}, bf16[2,128,1024]{1,2,0:T(8,128)(2,1)S(1)}, u32[]{:S(2)}, u32[]{:S(2)}) collective-permute-start(bf16[2,128,1024]{1,2,0:T(8,128)(2,1)S(1)} %pad_maximum_fusion.1), channel_id=1, source_target_pairs={{0,3},{1,4},{2,5},{3,6},{4,7},{5,8},{6,9},{7,10},{8,11},{9,12},{10... | collective-permute-start | bytes 1572872 | tf_op jit(solution)/shard_map/ppermute | solution.py:18
  20.4 31.2 %collective-permute-start.2 = (bf16[2,128,1024]{1,2,0:T(8,128)(2,1)S(1)}, bf16[2,128,1024]{1,2,0:T(8,128)(2,1)S(1)}, u32[]{:S(2)}, u32[]{:S(2)}) collective-permute-start(bf16[2,128,1024]{1,2,0:T(8,128)(2,1)S(1)} %pad_maximum_fusion.1), channel_id=1, source_target_pairs={{0,2},{1,3},{2,4},{3,5},{4,6},{5,7},{6,8},{7,9},{8,10},{9,11},{10,... | collective-permute-start | bytes 1572872 | tf_op jit(solution)/shard_map/ppermute | solution.py:18
  24.7 28.3 %collective-permute-start.3 = (bf16[2,128,1024]{1,2,0:T(8,128)(2,1)S(1)}, bf16[2,128,1024]{1,2,0:T(8,128)(2,1)S(1)}, u32[]{:S(2)}, u32[]{:S(2)}) collective-permute-start(bf16[2,128,1024]{1,2,0:T(8,128)(2,1)S(1)} %pad_maximum_fusion.1), channel_id=1, source_target_pairs={{0,1},{1,2},{2,3},{3,4},{4,5},{5,6},{6,7},{7,8},{8,9},{9,10},{10,1... | collective-permute-start | bytes 1572872 | tf_op jit(solution)/shard_map/ppermute | solution.py:18
  28.4 24.9 %collective-permute-start.4 = (bf16[2,128,1024]{1,2,0:T(8,128)(2,1)S(1)}, bf16[2,128,1024]{1,2,0:T(8,128)(2,1)S(1)}, u32[]{:S(2)}, u32[]{:S(2)}) collective-permute-start(bf16[2,128,1024]{1,2,0:T(8,128)(2,1)S(1)} %pad_maximum_fusion.1), channel_id=1, source_target_pairs={{1,0},{2,1},{3,2},{4,3},{5,4},{6,5},{7,6},{8,7},{9,8},{10,9},{11,1... | collective-permute-start | bytes 1572872 | tf_op jit(solution)/shard_map/ppermute | solution.py:18
  29.7 265.1 %reduce-scatter.2.cloned.1.call-start = ((), (), s32[]{:S(2)}) async-start(), calls=%async_computation.2 | async-start | bytes 4456448 | tf_op jit(solution)/shard_map/reduce_scatter | solution.py:108
  32.4 22.7 %collective-permute-start.5 = (bf16[2,128,1024]{1,2,0:T(8,128)(2,1)S(1)}, bf16[2,128,1024]{1,2,0:T(8,128)(2,1)S(1)}, u32[]{:S(2)}, u32[]{:S(2)}) collective-permute-start(bf16[2,128,1024]{1,2,0:T(8,128)(2,1)S(1)} %pad_maximum_fusion.1), channel_id=1, source_target_pairs={{2,0},{3,1},{4,2},{5,3},{6,4},{7,5},{8,6},{9,7},{10,8},{11,9},{12,... | collective-permute-start | bytes 1572872 | tf_op jit(solution)/shard_map/ppermute | solution.py:18
  41.5 34.7 %collective-permute-start.6 = (bf16[2,128,1024]{1,2,0:T(8,128)(2,1)S(1)}, bf16[2,128,1024]{1,2,0:T(8,128)(2,1)S(1)}, u32[]{:S(2)}, u32[]{:S(2)}) collective-permute-start(bf16[2,128,1024]{1,2,0:T(8,128)(2,1)S(1)} %pad_maximum_fusion.1), channel_id=1, source_target_pairs={{3,0},{4,1},{5,2},{6,3},{7,4},{8,5},{9,6},{10,7},{11,8},{12,9},{13... | collective-permute-start | bytes 1572872 | tf_op jit(solution)/shard_map/ppermute | solution.py:18
  51.6 55.3 %collective-permute-start.7 = (bf16[2,128,1024]{1,2,0:T(8,128)(2,1)S(1)}, bf16[2,128,1024]{1,2,0:T(8,128)(2,1)S(1)}, u32[]{:S(2)}, u32[]{:S(2)}) collective-permute-start(bf16[2,128,1024]{1,2,0:T(8,128)(2,1)S(1)} %pad_maximum_fusion.1), channel_id=1, source_target_pairs={{4,0},{5,1},{6,2},{7,3},{8,4},{9,5},{10,6},{11,7},{12,8},{13,9},{1... | collective-permute-start | bytes 1572872 | tf_op jit(solution)/shard_map/ppermute | solution.py:18
  109.6 29.0 %copy-start.7 = (bf16[1,128,1024]{2,1,0:T(8,128)(2,1)S(1)}, bf16[1,128,1024]{2,1,0:T(8,128)(2,1)}, u32[]{:S(2)}) copy-start(bf16[1,128,1024]{2,1,0:T(8,128)(2,1)} %param.22) | copy-start | bytes 786436
  141.4 438.1 %all-reduce.2.cloned.1.call-start = ((), (), s32[]{:S(2)}) async-start(), calls=%async_computation.3 | async-start | bytes 524288 | tf_op jit(solution)/shard_map/psum | solution.py:109
  151.9 10.7 %copy-start.2 = (bf16[128,256]{0,1:T(8,128)(2,1)}, bf16[128,256]{0,1:T(8,128)(2,1)S(1)}, u32[]{:S(2)}) copy-start(bf16[128,256]{0,1:T(8,128)(2,1)S(1)} %copy.54) | copy-start | bytes 196612 | tf_op jit(solution)/shard_map/while
  154.4 8.1 %copy-start.6 = (bf16[128,256]{0,1:T(8,128)(2,1)}, bf16[128,256]{0,1:T(8,128)(2,1)S(1)}, u32[]{:S(2)}) copy-start(bf16[128,256]{0,1:T(8,128)(2,1)S(1)} %constant_dynamic-slice_fusion.18) | copy-start | bytes 196612 | tf_op jit(solution)/shard_map/while
  175.8 10.7 %copy-start.2 = (bf16[128,256]{0,1:T(8,128)(2,1)}, bf16[128,256]{0,1:T(8,128)(2,1)S(1)}, u32[]{:S(2)}) copy-start(bf16[128,256]{0,1:T(8,128)(2,1)S(1)} %copy.54) | copy-start | bytes 196612 | tf_op jit(solution)/shard_map/while
  178.4 8.1 %copy-start.6 = (bf16[128,256]{0,1:T(8,128)(2,1)}, bf16[128,256]{0,1:T(8,128)(2,1)S(1)}, u32[]{:S(2)}) copy-start(bf16[128,256]{0,1:T(8,128)(2,1)S(1)} %constant_dynamic-slice_fusion.18) | copy-start | bytes 196612 | tf_op jit(solution)/shard_map/while
  199.4 10.7 %copy-start.2 = (bf16[128,256]{0,1:T(8,128)(2,1)}, bf16[128,256]{0,1:T(8,128)(2,1)S(1)}, u32[]{:S(2)}) copy-start(bf16[128,256]{0,1:T(8,128)(2,1)S(1)} %copy.54) | copy-start | bytes 196612 | tf_op jit(solution)/shard_map/while
  202.0 8.1 %copy-start.6 = (bf16[128,256]{0,1:T(8,128)(2,1)}, bf16[128,256]{0,1:T(8,128)(2,1)S(1)}, u32[]{:S(2)}) copy-start(bf16[128,256]{0,1:T(8,128)(2,1)S(1)} %constant_dynamic-slice_fusion.18) | copy-start | bytes 196612 | tf_op jit(solution)/shard_map/while
  223.0 10.7 %copy-start.2 = (bf16[128,256]{0,1:T(8,128)(2,1)}, bf16[128,256]{0,1:T(8,128)(2,1)S(1)}, u32[]{:S(2)}) copy-start(bf16[128,256]{0,1:T(8,128)(2,1)S(1)} %copy.54) | copy-start | bytes 196612 | tf_op jit(solution)/shard_map/while
  244.6 23.1 %copy-start.1 = (bf16[2,512,1024]{2,1,0:T(8,128)(2,1)S(1)}, bf16[2,512,1024]{2,1,0:T(8,128)(2,1)}, u32[]{:S(2)}) copy-start(bf16[2,512,1024]{2,1,0:T(8,128)(2,1)} %get-tuple-element.329) | copy-start | bytes 6291460
  247.3 46.3 %copy-start = (bf16[1024,1024]{1,0:T(8,128)(2,1)S(1)}, bf16[1024,1024]{1,0:T(8,128)(2,1)}, u32[]{:S(2)}) copy-start(bf16[1024,1024]{1,0:T(8,128)(2,1)} %all-gather.2.cloned.1.call-done) | copy-start | bytes 6291460
  247.3 46.3 %copy-start.5 = (bf16[128,1024]{0,1:T(8,128)(2,1)S(1)}, bf16[128,1024]{0,1:T(8,128)(2,1)}, u32[]{:S(2)}) copy-start(bf16[128,1024]{0,1:T(8,128)(2,1)} %copy-done.4) | copy-start | bytes 786436
  247.3 24.0 %collective-permute-start.15 = (bf16[2,128,1024]{2,1,0:T(8,128)(2,1)S(1)}, bf16[2,128,1024]{2,1,0:T(8,128)(2,1)S(1)}, u32[]{:S(2)}, u32[]{:S(2)}) collective-permute-start(bf16[2,128,1024]{2,1,0:T(8,128)(2,1)S(1)} %get-tuple-element.488), channel_id=1, source_target_pairs={{0,4},{1,5},{2,6},{3,7},{4,8},{5,9},{6,10},{7,11},{8,12},{9,13},{1... | collective-permute-start | bytes 1572872 | tf_op jit(solution)/shard_map/ppermute | solution.py:18
  258.9 23.6 %collective-permute-start.14 = (bf16[2,128,1024]{2,1,0:T(8,128)(2,1)S(1)}, bf16[2,128,1024]{2,1,0:T(8,128)(2,1)S(1)}, u32[]{:S(2)}, u32[]{:S(2)}) collective-permute-start(bf16[2,128,1024]{2,1,0:T(8,128)(2,1)S(1)} %get-tuple-element.486), channel_id=1, source_target_pairs={{0,3},{1,4},{2,5},{3,6},{4,7},{5,8},{6,9},{7,10},{8,11},{9,12},{10... | collective-permute-start | bytes 1572872 | tf_op jit(solution)/shard_map/ppermute | solution.py:18
  260.2 32.1 %collective-permute-start.13 = (bf16[2,128,1024]{2,1,0:T(8,128)(2,1)S(1)}, bf16[2,128,1024]{2,1,0:T(8,128)(2,1)S(1)}, u32[]{:S(2)}, u32[]{:S(2)}) collective-permute-start(bf16[2,128,1024]{2,1,0:T(8,128)(2,1)S(1)} %get-tuple-element.487), channel_id=1, source_target_pairs={{0,2},{1,3},{2,4},{3,5},{4,6},{5,7},{6,8},{7,9},{8,10},{9,11},{10,... | collective-permute-start | bytes 1572872 | tf_op jit(solution)/shard_map/ppermute | solution.py:18
  261.6 33.2 %collective-permute-start.12 = (bf16[2,128,1024]{2,1,0:T(8,128)(2,1)}, bf16[2,128,1024]{2,1,0:T(8,128)(2,1)S(1)}, u32[]{:S(2)}, u32[]{:S(2)}) collective-permute-start(bf16[2,128,1024]{2,1,0:T(8,128)(2,1)} %get-tuple-element.485), channel_id=1, source_target_pairs={{0,1},{1,2},{2,3},{3,4},{4,5},{5,6},{6,7},{7,8},{8,9},{9,10},{10,1... | collective-permute-start | bytes 1572872 | tf_op jit(solution)/shard_map/ppermute | solution.py:18
  269.0 43.5 %copy-start.3 = (f32[2,128,1024]{2,1,0:T(8,128)S(1)}, f32[2,128,1024]{2,1,0:T(8,128)}, u32[]{:S(2)}) copy-start(f32[2,128,1024]{2,1,0:T(8,128)} %get-tuple-element.328) | copy-start | bytes 3145732
  269.0 25.8 %collective-permute-start.11 = (bf16[2,128,1024]{2,1,0:T(8,128)(2,1)}, bf16[2,128,1024]{2,1,0:T(8,128)(2,1)}, u32[]{:S(2)}, u32[]{:S(2)}) collective-permute-start(bf16[2,128,1024]{2,1,0:T(8,128)(2,1)} %get-tuple-element.484), channel_id=1, source_target_pairs={{4,0},{5,1},{6,2},{7,3},{8,4},{9,5},{10,6},{11,7},{12,8},{13,9},{1... | collective-permute-start | bytes 1572872 | tf_op jit(solution)/shard_map/ppermute | solution.py:18
  271.2 30.3 %collective-permute-start.10 = (bf16[2,128,1024]{2,1,0:T(8,128)(2,1)}, bf16[2,128,1024]{2,1,0:T(8,128)(2,1)}, u32[]{:S(2)}, u32[]{:S(2)}) collective-permute-start(bf16[2,128,1024]{2,1,0:T(8,128)(2,1)} %get-tuple-element.482), channel_id=1, source_target_pairs={{3,0},{4,1},{5,2},{6,3},{7,4},{8,5},{9,6},{10,7},{11,8},{12,9},{13... | collective-permute-start | bytes 1572872 | tf_op jit(solution)/shard_map/ppermute | solution.py:18
  282.5 29.4 %collective-permute-start.9 = (bf16[2,128,1024]{2,1,0:T(8,128)(2,1)}, bf16[2,128,1024]{2,1,0:T(8,128)(2,1)}, u32[]{:S(2)}, u32[]{:S(2)}) collective-permute-start(bf16[2,128,1024]{2,1,0:T(8,128)(2,1)} %get-tuple-element.483), channel_id=1, source_target_pairs={{2,0},{3,1},{4,2},{5,3},{6,4},{7,5},{8,6},{9,7},{10,8},{11,9},{12,... | collective-permute-start | bytes 1572872 | tf_op jit(solution)/shard_map/ppermute | solution.py:18
  292.3 20.2 %collective-permute-start.8 = (bf16[2,128,1024]{2,1,0:T(8,128)(2,1)}, bf16[2,128,1024]{2,1,0:T(8,128)(2,1)}, u32[]{:S(2)}, u32[]{:S(2)}) collective-permute-start(bf16[2,128,1024]{2,1,0:T(8,128)(2,1)} %get-tuple-element.481), channel_id=1, source_target_pairs={{1,0},{2,1},{3,2},{4,3},{5,4},{6,5},{7,6},{8,7},{9,8},{10,9},{11,1... | collective-permute-start | bytes 1572872 | tf_op jit(solution)/shard_map/ppermute | solution.py:18
  (30 other events, 88.3 us)
Sparse Core Ops, SparseCore 0:
  29.9 76.8 all-gather.1
  141.5 109.0 reduce-scatter.1
  294.9 284.5 all-reduce.1
where the time goes:
time: 590 us; the launch traced here: 588 us
  waiting for transfers between devices  369 us (63%)
  matrix products  85.4 us (14%)
  local copies, waits for them, and re-layouts  56 us (9%)
  starting transfers between devices  49.9 us (8%)
  between operations  14.1 us (2%)
  other arithmetic  12.1 us (2%)
    psum x1, waiting for transfers between devices, body(): weight_sum = lax.psum(row_block, 'seq')  264 us
    ppermute x16, waiting for transfers between devices, shifted(): lax.ppermute(value, axis, [(source, source + steps) for source in range(f...  106 us
    ppermute x16, starting transfers between devices, shifted(): lax.ppermute(value, axis, [(source, source + steps) for source in range(f...  49.6 us
    dot_general x4, matrix products, backward_group(): jnp.einsum('hqk,qhd->khd', grad_score, query_grp, preferred_element_type=...  20.5 us
    sub x8, matrix products, soft_weights(): exponent = jnp.exp(scores - row_peak)  19 us
    dot_general x4, matrix products, backward_group(): jnp.einsum('hqk,khd->qhd', grad_score, key_grp, preferred_element_type=jn...  19 us
  transfers between devices with their start and end apart: 19, of which 12 were waited for; matrix products, arithmetic and copies ran while one was open for 25% of the time, Pallas kernels for 0%

commit v1 on v0

v1 whole, which is shorter than its diff:
```python
import math

import jax
import jax.numpy as jnp
from jax import lax
from jax.experimental import pallas as pl
from jax.experimental.pallas import tpu as pltpu
from jax.sharding import PartitionSpec as P

HEAD_DIM = 64
WINDOW = 512
BLOCK = 64
DOCS = 4
ROWS = 128
LANES = 128
SPAN = 9
SLOTS = 10
STEPS = 4
WIDTH = 1024
Z = 16
OFFSETS = (-2, -1, 1, 2)
MESH = pl.DeviceIdType.MESH
BF16 = jnp.bfloat16
F32 = jnp.float32

NT = (((1,), (1,)), ((), ()))
TN = (((0,), (0,)), ((), ()))


def dot(a, b, dims=(((1,), (0,)), ((), ()))):
    return lax.dot_general(a, b, dims, preferred_element_type=F32)


def remote(src, dst, send, recv, device):
    return pltpu.make_async_remote_copy(
        src_ref=src, dst_ref=dst, send_sem=send, recv_sem=recv, device_id=device, device_id_type=MESH
    )


def layer_kernel(
    lengths, upweight, q_in, k_in, v_in, ct_in, w_in,
    lo_out, dq_out, dk_out, dv_out, gw_out,
    qbuf, kv, ctb, gout, wbuf, bias, attbuf, attpair, dqb, acc, own, rout, rin, fin,
    gkeep, g1send, g1recv, g2send, g2recv, g2sum, g3send, g3recv, g4f, g4send, g4recv,
    zag, gwh, gwo, lob, s_scr, dp_scr, p_scr, ds_scr,
    l_sem, y_send, y_recv, ct_send, ct_recv, z_send, z_recv, wx_send, wx_recv, wc_send, wc_recv,
    wy_send, wy_recv, r_send, r_recv, a_send, a_recv, dq_send, dq_recv, f_send, f_recv, o_sem,
    g1_send, g1_rsem, g2_send, g2_rsem, g3_send, g3_rsem, g4_send, g4_rsem, g5_send, g5_rsem,
    g6_send, g6_rsem,
):
    d = lax.axis_index("doc")
    s = lax.axis_index("seq")
    z, y = s // 2, s % 2
    yh, x, core = d // 8, (d // 2) % 4, d % 2
    s_pair = z * 2 + (1 - y)
    d_core = yh * 8 + x * 2 + (1 - core)
    d_far = (1 - yh) * 8 + x * 2 + core

    def at_x(offset):
        return yh * 8 + ((x + offset + 4) % 4) * 2 + core

    def at_z(offset):
        return ((z + offset + Z) % Z) * 2 + y

    def pair_of(step):
        return (x + 3 - step) % 4

    def cols(column, step):
        return pl.ds(pl.multiple_of((column * 4 + pair_of(step)) * LANES, LANES), LANES)

    pair_dev = (d, s_pair)
    core_dev = (d_core, s)
    far_dev = (d_far, s_pair)

    barrier = pltpu.get_barrier_semaphore()
    partners = [pair_dev, core_dev, far_dev, (d_far, s)] + [(at_x(o), s) for o in (1, 2, 3)]
    for device in partners:
        pl.semaphore_signal(barrier, inc=1, device_id=device, device_id_type=MESH)

    def greet(o, carry):
        pl.semaphore_signal(barrier, inc=1, device_id=(d, at_z(o)), device_id_type=MESH)
        return carry

    lax.fori_loop(1, Z, greet, 0)
    pl.semaphore_wait(barrier, len(partners) + Z - 1)

    def own_copies(i):
        mine = cols(y, i)
        return [
            pltpu.make_async_copy(k_in.at[:, mine], kv.at[i, 4 + y, 0], l_sem.at[i, 0]),
            pltpu.make_async_copy(v_in.at[:, mine], kv.at[i, 4 + y, 1], l_sem.at[i, 1]),
            pltpu.make_async_copy(q_in.at[:, mine], qbuf.at[i, y], l_sem.at[i, 2]),
        ]

    def pair_copies(i):
        theirs = cols(1 - y, i)
        return [
            remote(k_in.at[:, theirs], kv.at[i, 4 + y, 0], y_send.at[i, 0], y_recv.at[i, 0], pair_dev),
            remote(v_in.at[:, theirs], kv.at[i, 4 + y, 1], y_send.at[i, 1], y_recv.at[i, 1], pair_dev),
            remote(q_in.at[:, theirs], qbuf.at[i, y], y_send.at[i, 2], y_recv.at[i, 2], pair_dev),
        ]

    def pair_arrivals(i):
        there = 5 - y
        return [
            remote(kv.at[i, there, 0], kv.at[i, there, 0], y_send.at[i, 0], y_recv.at[i, 0], pair_dev),
            remote(kv.at[i, there, 1], kv.at[i, there, 1], y_send.at[i, 1], y_recv.at[i, 1], pair_dev),
            remote(qbuf.at[i, 1 - y], qbuf.at[i, 1 - y], y_send.at[i, 2], y_recv.at[i, 2], pair_dev),
        ]

    def halo_copy(i, n):
        o = OFFSETS[n]
        return remote(
            kv.at[i, pl.ds(4, 2)], kv.at[i, pl.ds(4 - 2 * o, 2)], z_send.at[i, n], z_recv.at[i, n], (d, at_z(o))
        )

    def halo_arrival(i, n):
        o = OFFSETS[n]
        here = kv.at[i, pl.ds(4 - 2 * o, 2)]
        return remote(here, here, z_send.at[i, n], z_recv.at[i, n], (d, at_z(o)))

    own_ct = pltpu.make_async_copy(ct_in, ctb.at[y], l_sem.at[0, 3])
    own_w = pltpu.make_async_copy(w_in, wbuf.at[d], l_sem.at[1, 3])
    send_ct = remote(ct_in, ctb.at[y], ct_send, ct_recv, pair_dev)
    take_ct = remote(ctb.at[1 - y], ctb.at[1 - y], ct_send, ct_recv, pair_dev)

    for i in range(STEPS):
        for copy in own_copies(i)[:2]:
            copy.start()
        for copy in pair_copies(i)[:2]:
            copy.start()
    own_w.start()
    for o in (1, 2, 3):
        remote(w_in, wbuf.at[d], wx_send.at[o - 1], wx_recv.at[o - 1], (at_x(o), s)).start()
    for i in range(STEPS):
        own_copies(i)[2].start()
        pair_copies(i)[2].start()
    own_ct.start()
    send_ct.start()

    bounds = []
    total = jnp.int32(0)
    for j in range(DOCS):
        total = total + lengths[0, j] * BLOCK
        bounds.append(total)

    def doc_of(position):
        ids = jnp.zeros_like(position)
        for bound in bounds:
            ids = ids + (position >= bound).astype(jnp.int32)
        return ids

    for yp in range(2):
        base = (z * 2 + yp) * ROWS

        def fill(j, carry, yp=yp, base=base):
            rows = lax.broadcasted_iota(jnp.int32, (ROWS, ROWS), 0)
            lanes = lax.broadcasted_iota(jnp.int32, (ROWS, ROWS), 1)
            key = base - WINDOW + j * ROWS + rows
            query = base + lanes
            near = jnp.abs(query - key) <= WINDOW
            inside = (key >= 0) & (key < Z * 2 * ROWS)
            ok = near & inside & (doc_of(key) == doc_of(query))
            bias[yp, j] = jnp.where(ok, 0.0, -jnp.inf).astype(F32)
            return carry

        lax.fori_loop(0, SPAN, fill, 0)

    def pump(i, carry):
        for copy in own_copies(i)[:2]:
            copy.wait()
        for copy in pair_arrivals(i)[:2]:
            copy.wait_recv()
        for n in range(4):
            halo_copy(i, n).start()
        return carry

    lax.fori_loop(0, STEPS, pump, 0)

    def w_block(high, o):
        return wbuf.at[high * 8 + ((x - o + 4) % 4) * 2 + core]

    own_w.wait()
    for o in range(4):
        block = w_block(yh, o)
        if o:
            remote(block, block, wx_send.at[o - 1], wx_recv.at[o - 1], (at_x(-o), s)).wait_recv()
        remote(block, block, wy_send.at[o], wy_recv.at[o], far_dev).start()
        remote(block, block, wc_send.at[o], wc_recv.at[o], core_dev).start()

    own_ct.wait()
    take_ct.wait_recv()
    for yp in range(2):
        position = (z * 2 + yp) * ROWS + lax.broadcasted_iota(jnp.int32, (ROWS, LANES), 0)
        ids = doc_of(position)
        weight = jnp.zeros((ROWS, LANES), jnp.int32)
        for j in range(DOCS):
            weight = weight + jnp.where(ids == j, upweight[0, j], 0)
        weight = weight.astype(F32)
        for j in range(WIDTH // LANES):
            piece = slice(j * LANES, (j + 1) * LANES)
            gout[yp, :, piece] = (weight * ctb[yp, :, piece].astype(F32)).astype(BF16)

    for o in range(4):
        block = w_block(1 - yh, o)
        remote(block, block, wy_send.at[o], wy_recv.at[o], far_dev).wait_recv()
        remote(block, block, wc_send.at[4 + o], wc_recv.at[4 + o], core_dev).start()
    for o in range(4):
        for h, high in ((0, yh), (1, 1 - yh)):
            block = wbuf.at[high * 8 + ((x - o + 4) % 4) * 2 + (1 - core)]
            remote(block, block, wc_send.at[4 * h + o], wc_recv.at[4 * h + o], core_dev).wait_recv()

    for i in range(STEPS):
        own_copies(i)[2].wait()
        pair_arrivals(i)[2].wait_recv()

    lane = lax.broadcasted_iota(jnp.int32, (ROWS, LANES), 1)

    def stacked(block):
        block = block.astype(F32)
        low = jnp.where(lane < HEAD_DIM, block, 0.0).astype(BF16)
        high = jnp.where(lane >= HEAD_DIM, block, 0.0).astype(BF16)
        return jnp.concatenate([low, high], axis=0)

    def unstacked(block):
        return jnp.concatenate([block[:HEAD_DIM, :ROWS], block[HEAD_DIM:, ROWS:]], axis=0)

    def key_block(j):
        return slice(j * ROWS, (j + 1) * ROWS)

    def unit(i, yp, w_pair):
        query2 = stacked(qbuf[i, yp])
        grad2 = stacked(dot(gout[yp], w_pair, NT).astype(BF16))
        peak = jnp.full((8, 2 * ROWS), -jnp.inf, F32)
        for j in range(SPAN):
            mask = bias[yp, j]
            score = dot(kv[i, yp + j, 0], query2, NT) + jnp.concatenate([mask, mask], axis=1)
            s_scr[key_block(j)] = score
            peak = jnp.maximum(peak, jnp.max(score.reshape(ROWS // 8, 8, 2 * ROWS), axis=0))
        peak = jnp.max(peak, axis=0, keepdims=True)
        norm = jnp.zeros((8, 2 * ROWS), F32)
        centre = jnp.zeros((8, 2 * ROWS), F32)
        for j in range(SPAN):
            power = jnp.exp((s_scr[key_block(j)] - peak) * (HEAD_DIM ** -0.5))
            slope = dot(kv[i, yp + j, 1], grad2, NT)
            s_scr[key_block(j)] = power
            dp_scr[key_block(j)] = slope
            norm = norm + jnp.sum(power.reshape(ROWS // 8, 8, 2 * ROWS), axis=0)
            centre = centre + jnp.sum((power * slope).reshape(ROWS // 8, 8, 2 * ROWS), axis=0)
        share = 1.0 / jnp.sum(norm, axis=0, keepdims=True)
        centre = jnp.sum(centre, axis=0, keepdims=True) * share
        for j in range(SPAN):
            prob = s_scr[key_block(j)] * share
            half = prob.astype(BF16)
            grad_score = (prob * (dp_scr[key_block(j)] - centre) * (HEAD_DIM ** -0.5)).astype(BF16)
            p_scr[key_block(j)] = half
            ds_scr[key_block(j)] = grad_score
            key_part = dot(grad_score, query2)
            value_part = dot(half, grad2)
            if yp == 0:
                acc[j, 0] = key_part
                acc[j, 1] = value_part
            elif j + 1 < SPAN:
                acc[j + 1, 0] += key_part
                acc[j + 1, 1] += value_part
            else:
                acc[j + 1, 0] = key_part
                acc[j + 1, 1] = value_part
        keys = kv[i, yp:yp + SPAN, 0].reshape(SPAN * ROWS, LANES)
        values = kv[i, yp:yp + SPAN, 1].reshape(SPAN * ROWS, LANES)
        mixed = unstacked(dot(values, p_scr[...], TN))
        attpair[i, yp] = mixed.T.astype(BF16)
        dqb[i, yp] = unstacked(dot(keys, ds_scr[...], TN)).T.astype(BF16)
        return dot(mixed.astype(BF16), gout[yp])

    def att_send(i):
        return remote(
            attpair.at[i, 1 - y], attbuf.at[y * 4 + pair_of(i)], a_send.at[i], a_recv.at[i], pair_dev
        )

    def att_take(i):
        here = attbuf.at[(1 - y) * 4 + pair_of(i)]
        return remote(here, here, a_send.at[i], a_recv.at[i], pair_dev)

    def dq_own(i):
        return pltpu.make_async_copy(dqb.at[i, y], dq_out.at[:, cols(y, i)], o_sem.at[i, 0])

    def dq_pair(i):
        return remote(dqb.at[i, 1 - y], dq_out.at[:, cols(y, i)], dq_send.at[i], dq_recv.at[i], pair_dev)

    def dq_take(i):
        here = dq_out.at[:, cols(1 - y, i)]
        return remote(here, here, dq_send.at[i], dq_recv.at[i], pair_dev)

    def ret_copy(i, n):
        return remote(rout.at[i, n], rin.at[i, n], r_send.at[i, n], r_recv.at[i, n], (d, at_z(OFFSETS[n])))

    def g1_copy(i):
        return remote(g1send.at[i], g1recv.at[i], g1_send.at[i], g1_rsem.at[i], core_dev)

    def g2_copy(i):
        return remote(g2send.at[i], g2recv.at[i], g2_send.at[i], g2_rsem.at[i], (at_x(-1 - i), s))

    def g2_start(i):
        g1_copy(i).wait_recv()
        g2send[i] = (gkeep[i, core] + g1recv[i].astype(F32)).astype(BF16)
        g2_copy(i).start()

    def step(i, carry):
        for n in range(4):
            halo_arrival(i, n).wait_recv()
        doc_row = y * 8 + pair_of(i) * 2
        w_pair = wbuf[pl.ds(doc_row, 2)].reshape(2 * HEAD_DIM, WIDTH)
        weight_part = unit(i, 0, w_pair)
        weight_part = weight_part + unit(i, 1, w_pair)
        att_send(i).start()
        dq_own(i).start()
        dq_pair(i).start()
        attbuf[y * 4 + pair_of(i)] = attpair[i, y]
        for n in range(4):
            first = 4 + 2 * OFFSETS[n]
            rout[i, n] = acc[first:first + 2].astype(BF16)
            ret_copy(i, n).start()
        own[i] = acc[4:6]
        gkeep[i, 0] = weight_part[:HEAD_DIM]
        gkeep[i, 1] = weight_part[HEAD_DIM:]
        g1send[i] = gkeep[i, 1 - core].astype(BF16)
        g1_copy(i).start()

        @pl.when(i > 0)
        def _():
            g2_start(i - 1)

        return carry

    lax.fori_loop(0, STEPS, step, 0)

    g1_copy(3).wait_recv()
    head = gkeep[3, core] + g1recv[3].astype(F32)
    for i in range(3):
        remote(g2recv.at[i], g2recv.at[i], g2_send.at[i], g2_rsem.at[i], (at_x(1 + i), s)).wait_recv()
        head = head + g2recv[i].astype(F32)
    for j in range(8):
        g2sum[j] = head[:, j * LANES:(j + 1) * LANES]
    g3send[...] = g2sum[pl.ds((1 - yh) * 4, 4)].astype(BF16)
    g3 = remote(g3send, g3recv, g3_send, g3_rsem, (d_far, s))
    g3.start()

    def fin_own(i):
        return [
            pltpu.make_async_copy(fin.at[i, y, n], out.at[:, cols(y, i)], o_sem.at[i, 1 + n])
            for n, out in ((0, dk_out), (1, dv_out))
        ]

    def fin_pair(i):
        return [
            remote(fin.at[i, 1 - y, n], out.at[:, cols(y, i)], f_send.at[i, n], f_recv.at[i, n], pair_dev)
            for n, out in ((0, dk_out), (1, dv_out))
        ]

    def fin_take(i):
        views = [out.at[:, cols(1 - y, i)] for out in (dk_out, dv_out)]
        return [remote(views[n], views[n], f_send.at[i, n], f_recv.at[i, n], pair_dev) for n in range(2)]

    def finish(i):
        total = own[i]
        for n in range(4):
            ret_copy(i, n).wait_recv()
            total = total + rin[i, n].astype(F32)
        fin[i] = total.astype(BF16)
        for copy in fin_pair(i) + fin_own(i):
            copy.start()

    def finish_step(i, carry):
        finish(i)
        return carry

    lax.fori_loop(0, 2, finish_step, 0)

    g3.wait_recv()
    half_sum = g2sum[pl.ds(yh * 4, 4)] + g3recv[...].astype(F32)
    g4f[...] = half_sum.reshape(Z, 16, LANES)
    g4send[...] = g4f[...].astype(BF16)

    def g4_copy(o):
        return remote(
            g4send.at[(z + o) % Z], g4recv.at[o], g4_send.at[o], g4_rsem.at[o], (d, at_z(o))
        )

    def g4_start(o, carry):
        g4_copy(o).start()
        return carry

    lax.fori_loop(1, Z, g4_start, 0)

    for i in range(STEPS):
        att_take(i).wait_recv()
    rows = jnp.concatenate([attbuf[j] for j in range(8)], axis=1)
    for j in range(4):
        piece = slice(j * 256, (j + 1) * 256)
        lob[:, piece] = dot(rows, wbuf[:, :, piece].reshape(WIDTH, 256)).astype(BF16)
    lo_copy = pltpu.make_async_copy(lob, lo_out, o_sem.at[0, 3])
    lo_copy.start()

    def g4_wait(o, total):
        g4_copy(o).wait_recv()
        return total + g4recv[o].astype(F32)

    piece_sum = lax.fori_loop(1, Z, g4_wait, g4f[z])
    zag[z] = piece_sum * (1.0 / math.sqrt(Z * 2 * ROWS * 16))

    def g5_copy(o):
        return remote(zag.at[z], zag.at[z], g5_send.at[o], g5_rsem.at[o], (d, at_z(o)))

    def g5_take(o):
        here = zag.at[(z - o + Z) % Z]
        return remote(here, here, g5_send.at[o], g5_rsem.at[o], (d, at_z(o)))

    def g5_start(o, carry):
        g5_copy(o).start()
        return carry

    lax.fori_loop(1, Z, g5_start, 0)
    lax.fori_loop(2, STEPS, finish_step, 0)

    def g5_wait(o, carry):
        g5_take(o).wait_recv()
        return carry

    lax.fori_loop(1, Z, g5_wait, 0)

    def g6_copy(n, device):
        return remote(zag, gwh.at[yh], g6_send.at[n], g6_rsem.at[yh], device)

    def g6_take(part):
        return remote(gwh.at[part], gwh.at[part], g6_send.at[0], g6_rsem.at[part], pair_dev)

    @pl.when(yh == y)
    def _():
        g6_copy(0, pair_dev).start()
        gwh[yh] = zag[...]
        g6_take(1 - yh).wait_recv()
        g6_copy(0, pair_dev).wait_send()

    @pl.when(yh != y)
    def _():
        g6_copy(0, far_dev).start()
        g6_copy(1, (d_far, s)).start()
        g6_take(0).wait_recv()
        g6_take(1).wait_recv()
        g6_copy(0, far_dev).wait_send()
        g6_copy(1, (d_far, s)).wait_send()

    for part in range(2):
        for j in range(4):
            lanes = slice((part * 4 + j) * LANES, (part * 4 + j + 1) * LANES)
            gwo[:, lanes] = gwh[part, 4 * j:4 * j + 4].reshape(HEAD_DIM, LANES)
    gw_copy = pltpu.make_async_copy(gwo, gw_out, o_sem.at[1, 3])
    gw_copy.start()

    def drain(i, carry):
        for copy in pair_copies(i):
            copy.wait_send()
        for n in range(4):
            halo_copy(i, n).wait_send()
            ret_copy(i, n).wait_send()
        att_send(i).wait_send()
        dq_own(i).wait()
        dq_pair(i).wait_send()
        dq_take(i).wait_recv()
        g1_copy(i).wait_send()
        for copy in fin_own(i):
            copy.wait()
        for copy in fin_pair(i):
            copy.wait_send()
        for copy in fin_take(i):
            copy.wait_recv()
        return carry

    lax.fori_loop(0, STEPS, drain, 0)
    send_ct.wait_send()
    for o in (1, 2, 3):
        remote(w_in, wbuf.at[d], wx_send.at[o - 1], wx_recv.at[o - 1], (at_x(o), s)).wait_send()
        g2_copy(o - 1).wait_send()
    for o in range(4):
        block = w_block(yh, o)
        remote(block, block, wy_send.at[o], wy_recv.at[o], far_dev).wait_send()
        remote(block, block, wc_send.at[o], wc_recv.at[o], core_dev).wait_send()
        block = w_block(1 - yh, o)
        remote(block, block, wc_send.at[4 + o], wc_recv.at[4 + o], core_dev).wait_send()
    g3.wait_send()

    def drain_pieces(o, carry):
        g4_copy(o).wait_send()
        g5_copy(o).wait_send()
        return carry

    lax.fori_loop(1, Z, drain_pieces, 0)
    lo_copy.wait()
    gw_copy.wait()


def body(queries, key_rows, value_rows, cotangent, out_weight, lengths, upweight):
    vm = pltpu.VMEM
    dma = pltpu.SemaphoreType.DMA
    block = (ROWS, LANES)
    any_space = pl.BlockSpec(memory_space=pl.ANY)
    scalar = pl.BlockSpec(memory_space=pltpu.SMEM)
    rows_shape = jax.ShapeDtypeStruct((ROWS, WIDTH), BF16)
    outs = pl.pallas_call(
        layer_kernel,
        out_shape=(rows_shape,) * 4 + (jax.ShapeDtypeStruct((HEAD_DIM, WIDTH), F32),),
        in_specs=[scalar, scalar] + [any_space] * 5,
        out_specs=(any_space,) * 5,
        scratch_shapes=[
            vm((STEPS, 2) + block, BF16),
            vm((STEPS, SLOTS, 2) + block, BF16),
            vm((2, ROWS, WIDTH), BF16),
            vm((2, ROWS, WIDTH), BF16),
            vm((16, HEAD_DIM, WIDTH), BF16),
            vm((2, SPAN) + block, F32),
            vm((8,) + block, BF16),
            vm((STEPS, 2) + block, BF16),
            vm((STEPS, 2) + block, BF16),
            vm((SLOTS, 2) + block, F32),
            vm((STEPS, 2, 2) + block, F32),
            vm((STEPS, 4, 2, 2) + block, BF16),
            vm((STEPS, 4, 2, 2) + block, BF16),
            vm((STEPS, 2, 2) + block, BF16),
            vm((STEPS, 2, HEAD_DIM, WIDTH), F32),
            vm((STEPS, HEAD_DIM, WIDTH), BF16),
            vm((STEPS, HEAD_DIM, WIDTH), BF16),
            vm((3, HEAD_DIM, WIDTH), BF16),
            vm((3, HEAD_DIM, WIDTH), BF16),
            vm((8, HEAD_DIM, LANES), F32),
            vm((4, HEAD_DIM, LANES), BF16),
            vm((4, HEAD_DIM, LANES), BF16),
            vm((Z, 16, LANES), F32),
            vm((Z, 16, LANES), BF16),
            vm((Z, 16, LANES), BF16),
            vm((Z, 16, LANES), F32),
            vm((2, Z, 16, LANES), F32),
            vm((HEAD_DIM, WIDTH), F32),
            vm((ROWS, WIDTH), BF16),
            vm((SPAN * ROWS, 2 * ROWS), F32),
            vm((SPAN * ROWS, 2 * ROWS), F32),
            vm((SPAN * ROWS, 2 * ROWS), BF16),
            vm((SPAN * ROWS, 2 * ROWS), BF16),
            dma((STEPS, 4)),
            dma((STEPS, 3)), dma((STEPS, 3)),
            dma, dma,
            dma((STEPS, 4)), dma((STEPS, 4)),
            dma((3,)), dma((3,)),
            dma((8,)), dma((8,)),
            dma((4,)), dma((4,)),
            dma((STEPS, 4)), dma((STEPS, 4)),
            dma((STEPS,)), dma((STEPS,)),
            dma((STEPS,)), dma((STEPS,)),
            dma((STEPS, 2)), dma((STEPS, 2)),
            dma((STEPS, 4)),
            dma((STEPS,)), dma((STEPS,)),
            dma((3,)), dma((3,)),
            dma, dma,
            dma((Z,)), dma((Z,)),
            dma((Z,)), dma((Z,)),
            dma((2,)), dma((2,)),
        ],
        compiler_params=pltpu.CompilerParams(
            collective_id=0, has_side_effects=True, vmem_limit_bytes=56 * 2**20
        ),
        name="layer",
    )(lengths, upweight, queries[0], key_rows[0], value_rows[0], cotangent[0], out_weight)
    layer_out, grad_query, grad_key, grad_value, grad_weight = outs
    return (layer_out[None], grad_query[None], grad_key[None], grad_value[None], grad_weight)


def solution(mesh):
    rows = P("doc", "seq", None)
    flat = P("doc", None)
    return jax.shard_map(
        body,
        mesh=mesh,
        in_specs=(rows, rows, rows, rows, flat, flat, flat),
        out_specs=(rows, rows, rows, rows, flat),
        check_vma=False,
    )
```

time: 590 us -> 120 us (0.20)
  waiting for transfers between devices: 369 us -> 0 us
  Pallas kernels: 0 us -> 113 us
  matrix products: 85.4 us -> 0 us
  local copies, waits for them, and re-layouts: 56 us -> 5.55 us
  starting transfers between devices: 49.9 us -> 0 us
  between operations: 14.1 us -> 0.66 us
  other arithmetic: 12.1 us -> 0 us
    psum x1 -> x0, waiting for transfers between devices: 264 us -> none  [body(): weight_sum = lax.psum(row_block, 'seq')]
    pallas_call x0 -> x1, Pallas kernels: none -> 113 us  [body(): pl.pallas_call(layer_kernel, out_shape=(rows_shape,) * 4 + (jax.ShapeDtyp...]
    ppermute x16 -> x0, waiting for transfers between devices: 106 us -> none  [shifted(): lax.ppermute(value, axis, [(source, source + steps) for source in range(f...]
    dot_general x23 -> x0, matrix products: 66.3 us -> none  [the longest x4 20.5 us: backward_group(): jnp.einsum('hqk,qhd->khd', grad_score, query_grp, preferred_element_type=...]
    ppermute x16 -> x0, starting transfers between devices: 49.6 us -> none  [shifted(): lax.ppermute(value, axis, [(source, source + steps) for source in range(f...]
    dynamic_slice x28 -> x0, local copies, waits for them, and re-layouts: 25.2 us -> none  [the longest x8 9.92 us: group_slices(): lax.dynamic_slice_in_dim(key_ext, col_start, group_cols, 1)]
    sub x8 -> x0, matrix products: 19 us -> none  [soft_weights(): exponent = jnp.exp(scores - row_peak)]
    dynamic_update_slice x32 -> x0, local copies, waits for them, and re-layouts: 12.7 us -> none  [the longest x8 5.26 us: backward_group(): lax.dynamic_update_slice(later_grad, both_parts[:, WINDOW + rows_here:].a...]
  transfers between devices with their start and end apart: 19 -> 0, of which waited for: 12 -> 0; matrix products, arithmetic and copies ran while one was open for 25% -> 0% of each run, Pallas kernels for 0% -> 0%
where the time goes in v1:
time: 120 us
  Pallas kernels  113 us (94%)
  local copies, waits for them, and re-layouts  5.55 us (5%)
    pallas_call x1, Pallas kernels, body(): pl.pallas_call(layer_kernel, out_shape=(rows_shape,) * 4 + (jax.ShapeDtyp...  113 us
    unnamed x13, local copies, waits for them, and re-layouts  5.55 us

profile of v1, /device:TPU:6, one launch (start us, length us, event | category | flops | bytes accessed | tf_op | source)
XLA Modules:
  0.0 119.5 jit_solution(11369728452408111644)
XLA Ops:
  0.6 113.3 %layer.1 = (bf16[128,1024]{1,0:T(8,128)(2,1)}, bf16[128,1024]{1,0:T(8,128)(2,1)}, bf16[128,1024]{1,0:T(8,128)(2,1)}, bf16[128,1024]{1,0:T(8,128)(2,1)}, f32[64,1024]{1,0:T(8,128)}) custom-call(s32[1,4]{1,0:T(1,128)} %lengths.1, s32[1,4]{1,0:T(1,128)} %upweight.1, bf16[128,1024]{1,0:T(8,128)(2,1)} %bitcast.12, bf16[128,1024]{1,0:T(8,128)(2,1)} %bitcast.13, ...), custom_call_target="tpu_custom_call" | custom-call | tf_op jit(solution)/shard_map/layer/pallas_call | solution.py:510
  114.0 0.0 copy-start.3
  114.0 1.7 %copy.17 = bf16[1,128,1024]{2,1,0:T(8,128)(2,1)} copy(bf16[1,128,1024]{2,1,0:T(8,128)(2,1)} %bitcast.11) | data formatting | bytes 524288
  115.7 0.0 copy-done.3
  115.7 0.0 copy-start.2
  115.7 0.7 copy.18
  116.4 0.3 copy-done.2
  116.7 0.0 copy-start.1
  116.7 0.7 copy.19
  117.4 0.3 copy-done.1
  117.8 0.0 copy-start
  117.8 0.7 copy.20
  118.5 0.3 copy-done
  118.8 0.7 copy.21
Async XLA Ops:
  114.0 1.7 %copy-start.3 = (bf16[128,1024]{1,0:T(8,128)(2,1)S(1)}, bf16[128,1024]{1,0:T(8,128)(2,1)}, u32[]{:S(2)}) copy-start(bf16[128,1024]{1,0:T(8,128)(2,1)} %get-tuple-element.11) | copy-start | bytes 786436
  115.7 1.0 copy-start.2
  116.7 1.0 copy-start.1
  117.8 1.0 copy-start

commit v2 on v1

v2 whole, which is shorter than its diff:
```python
import math

import jax
import jax.numpy as jnp
from jax import lax
from jax.experimental import pallas as pl
from jax.experimental.pallas import tpu as pltpu
from jax.sharding import PartitionSpec as P

HEAD_DIM = 64
WINDOW = 512
BLOCK = 64
DOCS = 4
ROWS = 128
LANES = 128
SPAN = 9
SLOTS = 10
STEPS = 4
WIDTH = 1024
Z = 16
SIDES = (-1, 1)
MESH = pl.DeviceIdType.MESH
BF16 = jnp.bfloat16
F32 = jnp.float32

NT = (((1,), (1,)), ((), ()))
TN = (((0,), (0,)), ((), ()))


def dot(a, b, dims=(((1,), (0,)), ((), ()))):
    return lax.dot_general(a, b, dims, preferred_element_type=F32)


def remote(src, dst, send, recv, device):
    return pltpu.make_async_remote_copy(
        src_ref=src, dst_ref=dst, send_sem=send, recv_sem=recv, device_id=device, device_id_type=MESH
    )


def layer_kernel(
    lengths, upweight, q_in, k_in, v_in, ct_in, w_in,
    lo_out, dq_out, dk_out, dv_out, gw_out,
    qbuf, kv, ctb, gout, wbuf, bias, attbuf, attpair, dqb, acc, own, fout, fhere, rout, rin, fin,
    near, gkeep, g1send, g1recv, g2send, g2recv, g4f, g4send, g4recv, part, parts, zag, gwo, lob,
    s_scr, dp_scr, p_scr, ds_scr,
    l_sem, y_send, y_recv, ct_send, ct_recv, z_send, z_recv, zf_send, zf_recv, wx_send, wx_recv,
    wc_send, wc_recv, wy_send, wy_recv, r_send, r_recv, rf_send, rf_recv, a_send, a_recv,
    dq_send, dq_recv, f_send, f_recv, o_sem, g1_send, g1_rsem, g2_send, g2_rsem,
    g3_send, g3_rsem, g4_send, g4_rsem, g5_send, g5_rsem,
):
    d = lax.axis_index("doc")
    s = lax.axis_index("seq")
    z, y = s // 2, s % 2
    yh, x, core = d // 8, (d // 2) % 4, d % 2
    s_pair = z * 2 + (1 - y)
    d_core = yh * 8 + x * 2 + (1 - core)
    d_far = (1 - yh) * 8 + x * 2 + core

    def at_x(offset):
        return yh * 8 + ((x + offset + 4) % 4) * 2 + core

    def at_z(offset):
        return ((z + offset + Z) % Z) * 2 + y

    def pair_of(step):
        return (x + 3 - step) % 4

    def cols(column, step):
        return pl.ds(pl.multiple_of((column * 4 + pair_of(step)) * LANES, LANES), LANES)

    pair_dev = (d, s_pair)
    core_dev = (d_core, s)
    far_dev = (d_far, s_pair)

    barrier = pltpu.get_barrier_semaphore()
    partners = [pair_dev, core_dev, far_dev, (d_far, s)] + [(at_x(o), s) for o in (1, 2, 3)]
    for device in partners:
        pl.semaphore_signal(barrier, inc=1, device_id=device, device_id_type=MESH)

    def greet(o, carry):
        pl.semaphore_signal(barrier, inc=1, device_id=(d, at_z(o)), device_id_type=MESH)
        return carry

    lax.fori_loop(1, Z, greet, 0)
    pl.semaphore_wait(barrier, len(partners) + Z - 1)

    def own_kv(i):
        mine = cols(y, i)
        return [
            pltpu.make_async_copy(k_in.at[:, mine], kv.at[i, 4 + y, 0], l_sem.at[i, 0]),
            pltpu.make_async_copy(v_in.at[:, mine], kv.at[i, 4 + y, 1], l_sem.at[i, 1]),
        ]

    def own_q(i):
        return pltpu.make_async_copy(q_in.at[:, cols(y, i)], qbuf.at[i, y], l_sem.at[i, 2])

    def pair_kv(i):
        theirs = cols(1 - y, i)
        return [
            remote(k_in.at[:, theirs], kv.at[i, 4 + y, 0], y_send.at[i, 0], y_recv.at[i, 0], pair_dev),
            remote(v_in.at[:, theirs], kv.at[i, 4 + y, 1], y_send.at[i, 1], y_recv.at[i, 1], pair_dev),
        ]

    def pair_q(i):
        return remote(
            q_in.at[:, cols(1 - y, i)], qbuf.at[i, y], y_send.at[i, 2], y_recv.at[i, 2], pair_dev
        )

    def take_kv(i):
        views = [kv.at[i, 5 - y, n] for n in range(2)]
        return [remote(views[n], views[n], y_send.at[i, n], y_recv.at[i, n], pair_dev) for n in range(2)]

    def take_q(i):
        here = qbuf.at[i, 1 - y]
        return remote(here, here, y_send.at[i, 2], y_recv.at[i, 2], pair_dev)

    def halo(i, n, far, arrival=False):
        o = SIDES[n]
        to = 4 - 2 * o * (2 if far else 1)
        here = to if arrival else (4 - 2 * o if far else 4)
        send, recv = (zf_send, zf_recv) if far else (z_send, z_recv)
        return remote(
            kv.at[i, pl.ds(here, 2)], kv.at[i, pl.ds(to, 2)], send.at[i, n], recv.at[i, n], (d, at_z(o))
        )

    own_ct = pltpu.make_async_copy(ct_in, ctb.at[y], l_sem.at[0, 3])
    own_w = pltpu.make_async_copy(w_in, wbuf.at[d], l_sem.at[1, 3])
    send_ct = remote(ct_in, ctb.at[y], ct_send, ct_recv, pair_dev)
    take_ct = remote(ctb.at[1 - y], ctb.at[1 - y], ct_send, ct_recv, pair_dev)

    def start_kv(i):
        for copy in own_kv(i) + pair_kv(i):
            copy.start()

    def start_q(i):
        own_q(i).start()
        pair_q(i).start()

    def start_near(i):
        for copy in own_kv(i):
            copy.wait()
        for copy in take_kv(i):
            copy.wait_recv()
        for n in range(2):
            halo(i, n, False).start()

    def forward(i):
        for n in range(2):
            halo(i, n, False, True).wait_recv()
            halo(i, n, True).start()

    start_kv(0)
    start_kv(1)
    start_q(0)
    own_w.start()
    for o in (1, 2, 3):
        remote(w_in, wbuf.at[d], wx_send.at[o - 1], wx_recv.at[o - 1], (at_x(o), s)).start()
    own_ct.start()
    start_near(0)
    start_kv(2)
    start_q(1)
    start_near(1)
    start_kv(3)
    start_q(2)
    start_q(3)
    send_ct.start()

    bounds = []
    total = jnp.int32(0)
    for j in range(DOCS):
        total = total + lengths[0, j] * BLOCK
        bounds.append(total)

    def doc_of(position):
        ids = jnp.zeros_like(position)
        for bound in bounds:
            ids = ids + (position >= bound).astype(jnp.int32)
        return ids

    for yp in range(2):
        base = (z * 2 + yp) * ROWS

        def fill(j, carry, yp=yp, base=base):
            rows = lax.broadcasted_iota(jnp.int32, (ROWS, ROWS), 0)
            lanes = lax.broadcasted_iota(jnp.int32, (ROWS, ROWS), 1)
            key = base - WINDOW + j * ROWS + rows
            query = base + lanes
            near = jnp.abs(query - key) <= WINDOW
            inside = (key >= 0) & (key < Z * 2 * ROWS)
            ok = near & inside & (doc_of(key) == doc_of(query))
            bias[yp, j] = jnp.where(ok, 0.0, -jnp.inf).astype(F32)
            return carry

        lax.fori_loop(0, SPAN, fill, 0)

    def w_block(high, o):
        return wbuf.at[high * 8 + ((x - o + 4) % 4) * 2 + core]

    own_w.wait()
    for o in range(4):
        block = w_block(yh, o)
        if o:
            remote(block, block, wx_send.at[o - 1], wx_recv.at[o - 1], (at_x(-o), s)).wait_recv()
        remote(block, block, wy_send.at[o], wy_recv.at[o], far_dev).start()
        remote(block, block, wc_send.at[o], wc_recv.at[o], core_dev).start()

    forward(0)
    start_near(2)

    def grad_out_rows():
        own_ct.wait()
        take_ct.wait_recv()
        for yp in range(2):
            position = (z * 2 + yp) * ROWS + lax.broadcasted_iota(jnp.int32, (ROWS, LANES), 0)
            ids = doc_of(position)
            weight = jnp.zeros((ROWS, LANES), jnp.int32)
            for j in range(DOCS):
                weight = weight + jnp.where(ids == j, upweight[0, j], 0)
            weight = weight.astype(F32)
            for j in range(WIDTH // LANES):
                piece = slice(j * LANES, (j + 1) * LANES)
                gout[yp, :, piece] = (weight * ctb[yp, :, piece].astype(F32)).astype(BF16)

    def projection_rows():
        for o in range(4):
            block = w_block(1 - yh, o)
            remote(block, block, wy_send.at[o], wy_recv.at[o], far_dev).wait_recv()
            remote(block, block, wc_send.at[4 + o], wc_recv.at[4 + o], core_dev).start()
        for o in range(4):
            for h, high in ((0, yh), (1, 1 - yh)):
                block = wbuf.at[high * 8 + ((x - o + 4) % 4) * 2 + (1 - core)]
                remote(block, block, wc_send.at[4 * h + o], wc_recv.at[4 * h + o], core_dev).wait_recv()

    lane = lax.broadcasted_iota(jnp.int32, (ROWS, LANES), 1)

    def stacked(block):
        block = block.astype(F32)
        low = jnp.where(lane < HEAD_DIM, block, 0.0).astype(BF16)
        high = jnp.where(lane >= HEAD_DIM, block, 0.0).astype(BF16)
        return jnp.concatenate([low, high], axis=0)

    def unstacked(block):
        return jnp.concatenate([block[:HEAD_DIM, :ROWS], block[HEAD_DIM:, ROWS:]], axis=0)

    def key_block(j):
        return slice(j * ROWS, (j + 1) * ROWS)

    def ahead(i, yp):
        query2 = stacked(qbuf[i, yp])
        peak = jnp.full((8, 2 * ROWS), -jnp.inf, F32)
        for j in range(SPAN):
            mask = bias[yp, j]
            score = dot(kv[i, yp + j, 0], query2, NT) + jnp.concatenate([mask, mask], axis=1)
            s_scr[yp, key_block(j)] = score
            peak = jnp.maximum(peak, jnp.max(score.reshape(ROWS // 8, 8, 2 * ROWS), axis=0))
        peak = jnp.max(peak, axis=0, keepdims=True)
        norm = jnp.zeros((8, 2 * ROWS), F32)
        for j in range(SPAN):
            power = jnp.exp((s_scr[yp, key_block(j)] - peak) * (HEAD_DIM ** -0.5))
            s_scr[yp, key_block(j)] = power
            norm = norm + jnp.sum(power.reshape(ROWS // 8, 8, 2 * ROWS), axis=0)
        share = 1.0 / jnp.sum(norm, axis=0, keepdims=True)
        for j in range(SPAN):
            prob = s_scr[yp, key_block(j)] * share
            s_scr[yp, key_block(j)] = prob
            p_scr[yp, key_block(j)] = prob.astype(BF16)
        values = kv[i, yp:yp + SPAN, 1].reshape(SPAN * ROWS, LANES)
        mixed = unstacked(dot(values, p_scr[yp], TN))
        attpair[i, yp] = mixed.T.astype(BF16)
        return mixed.astype(BF16)

    def back(i, yp, w_pair):
        query2 = stacked(qbuf[i, yp])
        grad2 = stacked(dot(gout[yp], w_pair, NT).astype(BF16))
        centre = jnp.zeros((8, 2 * ROWS), F32)
        for j in range(SPAN):
            slope = dot(kv[i, yp + j, 1], grad2, NT)
            dp_scr[key_block(j)] = slope
            weighted = s_scr[yp, key_block(j)] * slope
            centre = centre + jnp.sum(weighted.reshape(ROWS // 8, 8, 2 * ROWS), axis=0)
        centre = jnp.sum(centre, axis=0, keepdims=True)
        for j in range(SPAN):
            prob = s_scr[yp, key_block(j)]
            grad_score = (prob * (dp_scr[key_block(j)] - centre) * (HEAD_DIM ** -0.5)).astype(BF16)
            ds_scr[key_block(j)] = grad_score
            key_part = dot(grad_score, query2)
            value_part = dot(p_scr[yp, key_block(j)], grad2)
            if yp == 0:
                acc[j, 0] = key_part
                acc[j, 1] = value_part
            elif j + 1 < SPAN:
                acc[j + 1, 0] += key_part
                acc[j + 1, 1] += value_part
            else:
                acc[j + 1, 0] = key_part
                acc[j + 1, 1] = value_part
        keys = kv[i, yp:yp + SPAN, 0].reshape(SPAN * ROWS, LANES)
        dqb[i, yp] = unstacked(dot(keys, ds_scr[...], TN)).T.astype(BF16)

    def att_send(i):
        return remote(
            attpair.at[i, 1 - y], attbuf.at[y * 4 + pair_of(i)], a_send.at[i], a_recv.at[i], pair_dev
        )

    def att_take(i):
        here = attbuf.at[(1 - y) * 4 + pair_of(i)]
        return remote(here, here, a_send.at[i], a_recv.at[i], pair_dev)

    def dq_own(i):
        return pltpu.make_async_copy(dqb.at[i, y], dq_out.at[:, cols(y, i)], o_sem.at[i, 0])

    def dq_pair(i):
        return remote(dqb.at[i, 1 - y], dq_out.at[:, cols(y, i)], dq_send.at[i], dq_recv.at[i], pair_dev)

    def dq_take(i):
        here = dq_out.at[:, cols(1 - y, i)]
        return remote(here, here, dq_send.at[i], dq_recv.at[i], pair_dev)

    def far_copy(i, n):
        return remote(fout.at[i, n], fhere.at[i, n], rf_send.at[i, n], rf_recv.at[i, n], (d, at_z(SIDES[n])))

    def ret_copy(i, n):
        return remote(rout.at[i, n], rin.at[i, n], r_send.at[i, n], r_recv.at[i, n], (d, at_z(SIDES[n])))

    def ret_start(i):
        for n in range(2):
            far_copy(i, n).wait_recv()
            rout[i, n] = (near[i, n] + fhere[i, n].astype(F32)).astype(BF16)
            ret_copy(i, n).start()

    def g1_copy(i):
        return remote(g1send.at[i], g1recv.at[i], g1_send.at[i], g1_rsem.at[i], core_dev)

    def g2_copy(i):
        return remote(g2send.at[i], g2recv.at[i], g2_send.at[i], g2_rsem.at[i], (at_x(-1 - i), s))

    def g2_start(i):
        g1_copy(i).wait_recv()
        g2send[i] = (gkeep[i, core] + g1recv[i].astype(F32)).astype(BF16)
        g2_copy(i).start()

    def fin_own(i):
        return [
            pltpu.make_async_copy(fin.at[i, y, n], out.at[:, cols(y, i)], o_sem.at[i, 1 + n])
            for n, out in ((0, dk_out), (1, dv_out))
        ]

    def fin_pair(i):
        return [
            remote(fin.at[i, 1 - y, n], out.at[:, cols(y, i)], f_send.at[i, n], f_recv.at[i, n], pair_dev)
            for n, out in ((0, dk_out), (1, dv_out))
        ]

    def fin_take(i):
        views = [out.at[:, cols(1 - y, i)] for out in (dk_out, dv_out)]
        return [remote(views[n], views[n], f_send.at[i, n], f_recv.at[i, n], pair_dev) for n in range(2)]

    def finish(i):
        total = own[i]
        for n in range(2):
            ret_copy(i, n).wait_recv()
            total = total + rin[i, n].astype(F32)
        fin[i] = total.astype(BF16)
        for copy in fin_pair(i) + fin_own(i):
            copy.start()

    def g4_copy(o):
        return remote(g4send.at[(z + o) % Z], g4recv.at[o], g4_send.at[o], g4_rsem.at[o], (d, at_z(o)))

    def head_sum():
        g1_copy(3).wait_recv()
        head = gkeep[3, core] + g1recv[3].astype(F32)
        for i in range(3):
            remote(g2recv.at[i], g2recv.at[i], g2_send.at[i], g2_rsem.at[i], (at_x(1 + i), s)).wait_recv()
            head = head + g2recv[i].astype(F32)
        for j in range(8):
            for half in range(2):
                g4f[2 * j + half] = head[half * 32:half * 32 + 32, j * LANES:(j + 1) * LANES]
        g4send[...] = g4f[...].astype(BF16)

        def g4_start(o, carry):
            g4_copy(o).start()
            return carry

        lax.fori_loop(1, Z, g4_start, 0)

    def step(i, carry):
        @pl.when(i < 3)
        def _():
            forward(i + 1)

        @pl.when(i == 0)
        def _():
            start_near(3)

        @pl.when(i > 0)
        def _():
            g2_start(i - 1)

        own_q(i).wait()
        take_q(i).wait_recv()
        for n in range(2):
            halo(i, n, True, True).wait_recv()
        mixed = [ahead(i, yp) for yp in range(2)]
        att_send(i).start()
        attbuf[y * 4 + pair_of(i)] = attpair[i, y]

        @pl.when(i == 0)
        def _():
            grad_out_rows()

        weight_part = dot(mixed[0], gout[0]) + dot(mixed[1], gout[1])
        gkeep[i, 0] = weight_part[:HEAD_DIM]
        gkeep[i, 1] = weight_part[HEAD_DIM:]
        g1send[i] = gkeep[i, 1 - core].astype(BF16)
        g1_copy(i).start()

        @pl.when(i == 0)
        def _():
            projection_rows()

        doc_row = y * 8 + pair_of(i) * 2
        w_pair = wbuf[pl.ds(doc_row, 2)].reshape(2 * HEAD_DIM, WIDTH)
        back(i, 0, w_pair)

        @pl.when(i == 3)
        def _():
            head_sum()

        back(i, 1, w_pair)
        for n in range(2):
            first = 8 * n
            fout[i, n] = acc[first:first + 2].astype(BF16)
            far_copy(i, n).start()
            near[i, n] = acc[2 + 4 * n:4 + 4 * n]
        own[i] = acc[4:6]
        dq_own(i).start()
        dq_pair(i).start()

        @pl.when(i > 0)
        def _():
            ret_start(i - 1)

        @pl.when(i > 1)
        def _():
            finish(i - 2)

        return carry

    lax.fori_loop(0, STEPS, step, 0)
    ret_start(3)
    finish(2)

    for i in range(STEPS):
        att_take(i).wait_recv()
    rows = jnp.concatenate([attbuf[j] for j in range(8)], axis=1)
    for j in range(4):
        piece = slice(j * 256, (j + 1) * 256)
        lob[:, piece] = dot(rows, wbuf[:, :, piece].reshape(WIDTH, 256)).astype(BF16)
    lo_copy = pltpu.make_async_copy(lob, lo_out, o_sem.at[0, 3])
    lo_copy.start()

    def g4_wait(o, total):
        g4_copy(o).wait_recv()
        return total + g4recv[o].astype(F32)

    part[...] = lax.fori_loop(1, Z, g4_wait, g4f[z])

    def g3_copy(n, device):
        slot = (yh + y) % 2
        return remote(part, parts.at[slot], g3_send.at[n], g3_rsem.at[slot], device)

    def g3_take(slot):
        return remote(parts.at[slot], parts.at[slot], g3_send.at[0], g3_rsem.at[slot], pair_dev)

    @pl.when(yh == y)
    def _():
        g3_copy(0, pair_dev).start()
        parts[0] = part[...]
        g3_take(1).wait_recv()
        g3_copy(0, pair_dev).wait_send()

    @pl.when(yh != y)
    def _():
        g3_copy(0, far_dev).start()
        g3_copy(1, (d_far, s)).start()
        g3_take(0).wait_recv()
        g3_take(1).wait_recv()
        g3_copy(0, far_dev).wait_send()
        g3_copy(1, (d_far, s)).wait_send()

    zag[z] = ((parts[0] + parts[1]) * (1.0 / math.sqrt(Z * 2 * ROWS * 16))).astype(BF16)

    def g5_copy(o):
        return remote(zag.at[z], zag.at[z], g5_send.at[o], g5_rsem.at[o], (d, at_z(o)))

    def g5_take(o):
        here = zag.at[(z - o + Z) % Z]
        return remote(here, here, g5_send.at[o], g5_rsem.at[o], (d, at_z(o)))

    def g5_start(o, carry):
        g5_copy(o).start()
        return carry

    lax.fori_loop(1, Z, g5_start, 0)
    finish(3)

    def g5_wait(o, carry):
        g5_take(o).wait_recv()
        return carry

    lax.fori_loop(1, Z, g5_wait, 0)
    for j in range(8):
        for half in range(2):
            gwo[half * 32:half * 32 + 32, j * LANES:(j + 1) * LANES] = zag[2 * j + half].astype(F32)
    gw_copy = pltpu.make_async_copy(gwo, gw_out, o_sem.at[1, 3])
    gw_copy.start()

    def drain(i, carry):
        for copy in pair_kv(i):
            copy.wait_send()
        pair_q(i).wait_send()
        for n in range(2):
            halo(i, n, False).wait_send()
            halo(i, n, True).wait_send()
            far_copy(i, n).wait_send()
            ret_copy(i, n).wait_send()
        att_send(i).wait_send()
        dq_own(i).wait()
        dq_pair(i).wait_send()
        dq_take(i).wait_recv()
        g1_copy(i).wait_send()
        for copy in fin_own(i):
            copy.wait()
        for copy in fin_pair(i):
            copy.wait_send()
        for copy in fin_take(i):
            copy.wait_recv()
        return carry

    lax.fori_loop(0, STEPS, drain, 0)
    send_ct.wait_send()
    for o in (1, 2, 3):
        remote(w_in, wbuf.at[d], wx_send.at[o - 1], wx_recv.at[o - 1], (at_x(o), s)).wait_send()
        g2_copy(o - 1).wait_send()
    for o in range(4):
        block = w_block(yh, o)
        remote(block, block, wy_send.at[o], wy_recv.at[o], far_dev).wait_send()
        remote(block, block, wc_send.at[o], wc_recv.at[o], core_dev).wait_send()
        block = w_block(1 - yh, o)
        remote(block, block, wc_send.at[4 + o], wc_recv.at[4 + o], core_dev).wait_send()

    def drain_pieces(o, carry):
        g4_copy(o).wait_send()
        g5_copy(o).wait_send()
        return carry

    lax.fori_loop(1, Z, drain_pieces, 0)
    lo_copy.wait()
    gw_copy.wait()


def copy_kernel(*refs):
    count = len(refs) // 2
    sems = refs[-1]
    copies = [pltpu.make_async_copy(refs[n], refs[count + n], sems.at[n]) for n in range(count)]
    for copy in copies:
        copy.start()
    for copy in copies:
        copy.wait()


def body(queries, key_rows, value_rows, cotangent, out_weight, lengths, upweight):
    vm = pltpu.VMEM
    dma = pltpu.SemaphoreType.DMA
    block = (ROWS, LANES)
    any_space = pl.BlockSpec(memory_space=pl.ANY)
    scalar = pl.BlockSpec(memory_space=pltpu.SMEM)
    rows_shape = jax.ShapeDtypeStruct((ROWS, WIDTH), BF16)
    outs = pl.pallas_call(
        layer_kernel,
        out_shape=(rows_shape,) * 4 + (jax.ShapeDtypeStruct((HEAD_DIM, WIDTH), F32),),
        in_specs=[scalar, scalar] + [any_space] * 5,
        out_specs=(any_space,) * 5,
        scratch_shapes=[
            vm((STEPS, 2) + block, BF16),
            vm((STEPS, SLOTS, 2) + block, BF16),
            vm((2, ROWS, WIDTH), BF16),
            vm((2, ROWS, WIDTH), BF16),
            vm((16, HEAD_DIM, WIDTH), BF16),
            vm((2, SPAN) + block, F32),
            vm((8,) + block, BF16),
            vm((STEPS, 2) + block, BF16),
            vm((STEPS, 2) + block, BF16),
            vm((SLOTS, 2) + block, F32),
            vm((STEPS, 2, 2) + block, F32),
            vm((STEPS, 2, 2, 2) + block, BF16),
            vm((STEPS, 2, 2, 2) + block, BF16),
            vm((STEPS, 2, 2, 2) + block, BF16),
            vm((STEPS, 2, 2, 2) + block, BF16),
            vm((STEPS, 2, 2) + block, BF16),
            vm((STEPS, 2, 2, 2) + block, F32),
            vm((STEPS, 2, HEAD_DIM, WIDTH), F32),
            vm((STEPS, HEAD_DIM, WIDTH), BF16),
            vm((STEPS, HEAD_DIM, WIDTH), BF16),
            vm((3, HEAD_DIM, WIDTH), BF16),
            vm((3, HEAD_DIM, WIDTH), BF16),
            vm((Z, 32, LANES), F32),
            vm((Z, 32, LANES), BF16),
            vm((Z, 32, LANES), BF16),
            vm((32, LANES), F32),
            vm((2, 32, LANES), F32),
            vm((Z, 32, LANES), BF16),
            vm((HEAD_DIM, WIDTH), F32),
            vm((ROWS, WIDTH), BF16),
            vm((2, SPAN * ROWS, 2 * ROWS), F32),
            vm((SPAN * ROWS, 2 * ROWS), F32),
            vm((2, SPAN * ROWS, 2 * ROWS), BF16),
            vm((SPAN * ROWS, 2 * ROWS), BF16),
            dma((STEPS, 4)),
            dma((STEPS, 3)), dma((STEPS, 3)),
            dma, dma,
            dma((STEPS, 2)), dma((STEPS, 2)),
            dma((STEPS, 2)), dma((STEPS, 2)),
            dma((3,)), dma((3,)),
            dma((8,)), dma((8,)),
            dma((4,)), dma((4,)),
            dma((STEPS, 2)), dma((STEPS, 2)),
            dma((STEPS, 2)), dma((STEPS, 2)),
            dma((STEPS,)), dma((STEPS,)),
            dma((STEPS,)), dma((STEPS,)),
            dma((STEPS, 2)), dma((STEPS, 2)),
            dma((STEPS, 4)),
            dma((STEPS,)), dma((STEPS,)),
            dma((3,)), dma((3,)),
            dma((2,)), dma((2,)),
            dma((Z,)), dma((Z,)),
            dma((Z,)), dma((Z,)),
        ],
        compiler_params=pltpu.CompilerParams(
            collective_id=0, has_side_effects=True, vmem_limit_bytes=56 * 2**20
        ),
        name="layer",
    )(lengths, upweight, queries[0], key_rows[0], value_rows[0], cotangent[0], out_weight)
    outs = pl.pallas_call(
        copy_kernel,
        out_shape=tuple(jax.ShapeDtypeStruct(a.shape, a.dtype) for a in outs),
        in_specs=[any_space] * 5,
        out_specs=(any_space,) * 5,
        scratch_shapes=[dma((5,))],
        name="outputs",
    )(*outs)
    layer_out, grad_query, grad_key, grad_value, grad_weight = outs
    return (layer_out[None], grad_query[None], grad_key[None], grad_value[None], grad_weight)


def solution(mesh):
    rows = P("doc", "seq", None)
    flat = P("doc", None)
    return jax.shard_map(
        body,
        mesh=mesh,
        in_specs=(rows, rows, rows, rows, flat, flat, flat),
        out_specs=(rows, rows, rows, rows, flat),
        check_vma=False,
    )
```

time: 120 us -> 132 us (1.10)
  Pallas kernels: 113 us -> 132 us
  local copies, waits for them, and re-layouts: 5.55 us -> 0 us
    pallas_call x0 -> x1, Pallas kernels: none -> 40.9 us  [body(): pl.pallas_call(copy_kernel, out_shape=tuple((jax.ShapeDtypeStruct(a.shape...]
    pallas_call x1, Pallas kernels: 113 us -> 90.7 us  [body(): pl.pallas_call(layer_kernel, out_shape=(rows_shape,) * 4 + (jax.ShapeDtyp...]
    unnamed x13 -> x0, local copies, waits for them, and re-layouts: 5.55 us -> none
where the time goes in v2:
time: 132 us
  Pallas kernels  132 us (100%)
    pallas_call x1, Pallas kernels, body(): pl.pallas_call(layer_kernel, out_shape=(rows_shape,) * 4 + (jax.ShapeDtyp...  90.7 us
    pallas_call x1, Pallas kernels, body(): pl.pallas_call(copy_kernel, out_shape=tuple((jax.ShapeDtypeStruct(a.shape...  40.9 us

profile of v2, /device:TPU:6, one launch (start us, length us, event | category | flops | bytes accessed | tf_op | source)
XLA Modules:
  0.0 132.2 jit_solution(7603269417988804213)
XLA Ops:
  0.6 90.7 %layer.1 = (bf16[128,1024]{1,0:T(8,128)(2,1)}, bf16[128,1024]{1,0:T(8,128)(2,1)}, bf16[128,1024]{1,0:T(8,128)(2,1)}, bf16[128,1024]{1,0:T(8,128)(2,1)}, f32[64,1024]{1,0:T(8,128)}) custom-call(s32[1,4]{1,0:T(1,128)} %lengths.1, s32[1,4]{1,0:T(1,128)} %upweight.1, bf16[128,1024]{1,0:T(8,128)(2,1)} %bitcast.8, bf16[128,1024]{1,0:T(8,128)(2,1)} %bitcast.9, ...), custom_call_target="tpu_custom_call" | custom-call | tf_op jit(solution)/shard_map/layer/pallas_call | solution.py:580
  91.3 40.9 %outputs.1 = (bf16[128,1024]{1,0:T(8,128)(2,1)}, bf16[128,1024]{1,0:T(8,128)(2,1)}, bf16[128,1024]{1,0:T(8,128)(2,1)}, bf16[128,1024]{1,0:T(8,128)(2,1)}, f32[64,1024]{1,0:T(8,128)}) custom-call(bf16[128,1024]{1,0:T(8,128)(2,1)} %get-tuple-element.15.refs_0_, bf16[128,1024]{1,0:T(8,128)(2,1)} %get-tuple-element.16.refs_1_, ...), custom_call_target="tpu_custom_call" | custom-call | tf_op jit(solution)/shard_map/outputs/pallas_call | solution.py:645

commit v3 on v2

--- a/solution.py
+++ b/solution.py
@@ -561,13 +561,16 @@
 
 
 def copy_kernel(*refs):
-    count = len(refs) // 2
-    sems = refs[-1]
-    copies = [pltpu.make_async_copy(refs[n], refs[count + n], sems.at[n]) for n in range(count)]
-    for copy in copies:
-        copy.start()
-    for copy in copies:
-        copy.wait()
+    sources, targets, rooms, sems = refs[:5], refs[5:10], refs[10:15], refs[15]
+    loads = [pltpu.make_async_copy(sources[n], rooms[n], sems.at[n]) for n in range(5)]
+    stores = [pltpu.make_async_copy(rooms[n], targets[n], sems.at[5 + n]) for n in range(5)]
+    for load in loads:
+        load.start()
+    for load, store in zip(loads, stores):
+        load.wait()
+        store.start()
+    for store in stores:
+        store.wait()
 
 
 def body(queries, key_rows, value_rows, cotangent, out_weight, lengths, upweight):
@@ -647,7 +650,7 @@
         out_shape=tuple(jax.ShapeDtypeStruct(a.shape, a.dtype) for a in outs),
         in_specs=[any_space] * 5,
         out_specs=(any_space,) * 5,
-        scratch_shapes=[dma((5,))],
+        scratch_shapes=[vm(a.shape, a.dtype) for a in outs] + [dma((10,))],
         name="outputs",
     )(*outs)
     layer_out, grad_query, grad_key, grad_value, grad_weight = outs

time: 132 us -> 93.6 us (0.71)
  Pallas kernels: 132 us -> 92.8 us
    pallas_call x1, Pallas kernels: 40.9 us -> 2.09 us  [body(): pl.pallas_call(copy_kernel, out_shape=tuple((jax.ShapeDtypeStruct(a.shape...]
where the time goes in v3:
time: 93.6 us; the launch traced here: 93.4 us
  Pallas kernels  92.8 us (99%)
    pallas_call x1, Pallas kernels, body(): pl.pallas_call(layer_kernel, out_shape=(rows_shape,) * 4 + (jax.ShapeDtyp...  90.7 us
    pallas_call x1, Pallas kernels, body(): pl.pallas_call(copy_kernel, out_shape=tuple((jax.ShapeDtypeStruct(a.shape...  2.09 us

profile of v3, /device:TPU:6, one launch (start us, length us, event | category | flops | bytes accessed | tf_op | source)
XLA Modules:
  0.0 93.4 jit_solution(1366109069989622800)
XLA Ops:
  0.6 90.7 %layer.1 = (bf16[128,1024]{1,0:T(8,128)(2,1)}, bf16[128,1024]{1,0:T(8,128)(2,1)}, bf16[128,1024]{1,0:T(8,128)(2,1)}, bf16[128,1024]{1,0:T(8,128)(2,1)}, f32[64,1024]{1,0:T(8,128)}) custom-call(s32[1,4]{1,0:T(1,128)} %lengths.1, s32[1,4]{1,0:T(1,128)} %upweight.1, bf16[128,1024]{1,0:T(8,128)(2,1)} %bitcast.8, bf16[128,1024]{1,0:T(8,128)(2,1)} %bitcast.9, ...), custom_call_target="tpu_custom_call" | custom-call | tf_op jit(solution)/shard_map/layer/pallas_call | solution.py:583
  91.3 2.1 %outputs.1 = (bf16[128,1024]{1,0:T(8,128)(2,1)}, bf16[128,1024]{1,0:T(8,128)(2,1)}, bf16[128,1024]{1,0:T(8,128)(2,1)}, bf16[128,1024]{1,0:T(8,128)(2,1)}, f32[64,1024]{1,0:T(8,128)}) custom-call(bf16[128,1024]{1,0:T(8,128)(2,1)} %get-tuple-element.15.refs_0_, bf16[128,1024]{1,0:T(8,128)(2,1)} %get-tuple-element.16.refs_1_, ...), custom_call_target="tpu_custom_call" | custom-call | tf_op jit(solution)/shard_map/outputs/pallas_call | solution.py:648

commit v4 on v3

--- a/solution.py
+++ b/solution.py
@@ -251,23 +251,22 @@
         for j in range(SPAN):
             mask = bias[yp, j]
             score = dot(kv[i, yp + j, 0], query2, NT) + jnp.concatenate([mask, mask], axis=1)
-            s_scr[yp, key_block(j)] = score
+            s_scr[i % 2, yp, key_block(j)] = score
             peak = jnp.maximum(peak, jnp.max(score.reshape(ROWS // 8, 8, 2 * ROWS), axis=0))
         peak = jnp.max(peak, axis=0, keepdims=True)
         norm = jnp.zeros((8, 2 * ROWS), F32)
         for j in range(SPAN):
-            power = jnp.exp((s_scr[yp, key_block(j)] - peak) * (HEAD_DIM ** -0.5))
-            s_scr[yp, key_block(j)] = power
+            power = jnp.exp((s_scr[i % 2, yp, key_block(j)] - peak) * (HEAD_DIM ** -0.5))
+            s_scr[i % 2, yp, key_block(j)] = power
             norm = norm + jnp.sum(power.reshape(ROWS // 8, 8, 2 * ROWS), axis=0)
         share = 1.0 / jnp.sum(norm, axis=0, keepdims=True)
         for j in range(SPAN):
-            prob = s_scr[yp, key_block(j)] * share
-            s_scr[yp, key_block(j)] = prob
-            p_scr[yp, key_block(j)] = prob.astype(BF16)
+            prob = s_scr[i % 2, yp, key_block(j)] * share
+            s_scr[i % 2, yp, key_block(j)] = prob
+            p_scr[i % 2, yp, key_block(j)] = prob.astype(BF16)
         values = kv[i, yp:yp + SPAN, 1].reshape(SPAN * ROWS, LANES)
-        mixed = unstacked(dot(values, p_scr[yp], TN))
+        mixed = unstacked(dot(values, p_scr[i % 2, yp], TN))
         attpair[i, yp] = mixed.T.astype(BF16)
-        return mixed.astype(BF16)
 
     def back(i, yp, w_pair):
         query2 = stacked(qbuf[i, yp])
@@ -276,15 +275,15 @@
         for j in range(SPAN):
             slope = dot(kv[i, yp + j, 1], grad2, NT)
             dp_scr[key_block(j)] = slope
-            weighted = s_scr[yp, key_block(j)] * slope
+            weighted = s_scr[i % 2, yp, key_block(j)] * slope
             centre = centre + jnp.sum(weighted.reshape(ROWS // 8, 8, 2 * ROWS), axis=0)
         centre = jnp.sum(centre, axis=0, keepdims=True)
         for j in range(SPAN):
-            prob = s_scr[yp, key_block(j)]
+            prob = s_scr[i % 2, yp, key_block(j)]
             grad_score = (prob * (dp_scr[key_block(j)] - centre) * (HEAD_DIM ** -0.5)).astype(BF16)
             ds_scr[key_block(j)] = grad_score
             key_part = dot(grad_score, query2)
-            value_part = dot(p_scr[yp, key_block(j)], grad2)
+            value_part = dot(p_scr[i % 2, yp, key_block(j)], grad2)
             if yp == 0:
                 acc[j, 0] = key_part
                 acc[j, 1] = value_part
@@ -384,49 +383,68 @@
 
         lax.fori_loop(1, Z, g4_start, 0)
 
-    def step(i, carry):
-        @pl.when(i < 3)
-        def _():
-            forward(i + 1)
-
-        @pl.when(i == 0)
-        def _():
-            start_near(3)
-
-        @pl.when(i > 0)
-        def _():
-            g2_start(i - 1)
-
-        own_q(i).wait()
-        take_q(i).wait_recv()
-        for n in range(2):
-            halo(i, n, True, True).wait_recv()
-        mixed = [ahead(i, yp) for yp in range(2)]
-        att_send(i).start()
-        attbuf[y * 4 + pair_of(i)] = attpair[i, y]
-
-        @pl.when(i == 0)
-        def _():
-            grad_out_rows()
-
-        weight_part = dot(mixed[0], gout[0]) + dot(mixed[1], gout[1])
+    def weigh(i):
+        weight_part = dot(attpair[i, 0], gout[0], TN) + dot(attpair[i, 1], gout[1], TN)
         gkeep[i, 0] = weight_part[:HEAD_DIM]
         gkeep[i, 1] = weight_part[HEAD_DIM:]
         g1send[i] = gkeep[i, 1 - core].astype(BF16)
         g1_copy(i).start()
 
+    def step(i, carry):
+        @pl.when(i < 3)
+        def _():
+            forward(i + 1)
+
         @pl.when(i == 0)
         def _():
+            start_near(3)
+
+        @pl.when(i == 2)
+        def _():
+            g2_start(0)
+
+        @pl.when((i > 1) & (i < STEPS))
+        def _():
+            g2_start(i - 1)
+
+        @pl.when(i < STEPS)
+        def _():
+            own_q(i).wait()
+            take_q(i).wait_recv()
+            for n in range(2):
+                halo(i, n, True, True).wait_recv()
+            for yp in range(2):
+                ahead(i, yp)
+            att_send(i).start()
+            attbuf[y * 4 + pair_of(i)] = attpair[i, y]
+
+        @pl.when(i == 1)
+        def _():
+            grad_out_rows()
+            weigh(0)
+
+        @pl.when((i > 0) & (i < STEPS))
+        def _():
+            weigh(i)
+
+        @pl.when(i == 1)
+        def _():
             projection_rows()
 
+        @pl.when(i == STEPS)
+        def _():
+            head_sum()
+
+        @pl.when(i > 0)
+        def _():
+            behind(i - 1)
+
+        return carry
+
+    def behind(i):
         doc_row = y * 8 + pair_of(i) * 2
         w_pair = wbuf[pl.ds(doc_row, 2)].reshape(2 * HEAD_DIM, WIDTH)
         back(i, 0, w_pair)
-
-        @pl.when(i == 3)
-        def _():
-            head_sum()
-
         back(i, 1, w_pair)
         for n in range(2):
             first = 8 * n
@@ -445,9 +463,7 @@
         def _():
             finish(i - 2)
 
-        return carry
-
-    lax.fori_loop(0, STEPS, step, 0)
+    lax.fori_loop(0, STEPS + 1, step, 0)
     ret_start(3)
     finish(2)
 
@@ -616,9 +632,9 @@
             vm((Z, 32, LANES), BF16),
             vm((HEAD_DIM, WIDTH), F32),
             vm((ROWS, WIDTH), BF16),
-            vm((2, SPAN * ROWS, 2 * ROWS), F32),
+            vm((2, 2, SPAN * ROWS, 2 * ROWS), F32),
             vm((SPAN * ROWS, 2 * ROWS), F32),
-            vm((2, SPAN * ROWS, 2 * ROWS), BF16),
+            vm((2, 2, SPAN * ROWS, 2 * ROWS), BF16),
             vm((SPAN * ROWS, 2 * ROWS), BF16),
             dma((STEPS, 4)),
             dma((STEPS, 3)), dma((STEPS, 3)),

time: 93.6 us -> 95.1 us (1.016)
  the two profiles are of different devices: /device:TPU:6 before, /device:TPU:1 now
where the time goes in v4:
time: 95.1 us; the launch traced here: 95 us
  Pallas kernels  94.3 us (99%)
    pallas_call x1, Pallas kernels, body(): pl.pallas_call(layer_kernel, out_shape=(rows_shape,) * 4 + (jax.ShapeDtyp...  92.2 us
    pallas_call x1, Pallas kernels, body(): pl.pallas_call(copy_kernel, out_shape=tuple((jax.ShapeDtypeStruct(a.shape...  2.09 us

profile of v4, /device:TPU:1, one launch (start us, length us, event | category | flops | bytes accessed | tf_op | source)
XLA Modules:
  0.0 95.0 jit_solution(12839317080750281643)
XLA Ops:
  0.6 92.2 %layer.1 = (bf16[128,1024]{1,0:T(8,128)(2,1)}, bf16[128,1024]{1,0:T(8,128)(2,1)}, bf16[128,1024]{1,0:T(8,128)(2,1)}, bf16[128,1024]{1,0:T(8,128)(2,1)}, f32[64,1024]{1,0:T(8,128)}) custom-call(s32[1,4]{1,0:T(1,128)} %lengths.1, s32[1,4]{1,0:T(1,128)} %upweight.1, bf16[128,1024]{1,0:T(8,128)(2,1)} %bitcast.8, bf16[128,1024]{1,0:T(8,128)(2,1)} %bitcast.9, ...), custom_call_target="tpu_custom_call" | custom-call | tf_op jit(solution)/shard_map/layer/pallas_call | solution.py:599
  92.9 2.1 %outputs.1 = (bf16[128,1024]{1,0:T(8,128)(2,1)}, bf16[128,1024]{1,0:T(8,128)(2,1)}, bf16[128,1024]{1,0:T(8,128)(2,1)}, bf16[128,1024]{1,0:T(8,128)(2,1)}, f32[64,1024]{1,0:T(8,128)}) custom-call(bf16[128,1024]{1,0:T(8,128)(2,1)} %get-tuple-element.15.refs_0_, bf16[128,1024]{1,0:T(8,128)(2,1)} %get-tuple-element.16.refs_1_, ...), custom_call_target="tpu_custom_call" | custom-call | tf_op jit(solution)/shard_map/outputs/pallas_call | solution.py:664

commit v5 on v4

--- a/solution.py
+++ b/solution.py
@@ -19,6 +19,7 @@
 WIDTH = 1024
 Z = 16
 SIDES = (-1, 1)
+OFFSETS = (-2, -1, 1, 2)
 MESH = pl.DeviceIdType.MESH
 BF16 = jnp.bfloat16
 F32 = jnp.float32
@@ -40,11 +41,11 @@
 def layer_kernel(
     lengths, upweight, q_in, k_in, v_in, ct_in, w_in,
     lo_out, dq_out, dk_out, dv_out, gw_out,
-    qbuf, kv, ctb, gout, wbuf, bias, attbuf, attpair, dqb, acc, own, fout, fhere, rout, rin, fin,
-    near, gkeep, g1send, g1recv, g2send, g2recv, g4f, g4send, g4recv, part, parts, zag, gwo, lob,
+    qbuf, kv, ctb, gout, wbuf, bias, attbuf, attpair, dqb, acc, own, rout, rin, fin,
+    gkeep, g1send, g1recv, g2send, g2recv, g4f, g4send, g4recv, part, parts, zag, gwo, lob,
     s_scr, dp_scr, p_scr, ds_scr,
     l_sem, y_send, y_recv, ct_send, ct_recv, z_send, z_recv, zf_send, zf_recv, wx_send, wx_recv,
-    wc_send, wc_recv, wy_send, wy_recv, r_send, r_recv, rf_send, rf_recv, a_send, a_recv,
+    wc_send, wc_recv, wy_send, wy_recv, r_send, r_recv, a_send, a_recv,
     dq_send, dq_recv, f_send, f_recv, o_sem, g1_send, g1_rsem, g2_send, g2_rsem,
     g3_send, g3_rsem, g4_send, g4_rsem, g5_send, g5_rsem,
 ):
@@ -315,17 +316,8 @@
         here = dq_out.at[:, cols(1 - y, i)]
         return remote(here, here, dq_send.at[i], dq_recv.at[i], pair_dev)
 
-    def far_copy(i, n):
-        return remote(fout.at[i, n], fhere.at[i, n], rf_send.at[i, n], rf_recv.at[i, n], (d, at_z(SIDES[n])))
-
     def ret_copy(i, n):
-        return remote(rout.at[i, n], rin.at[i, n], r_send.at[i, n], r_recv.at[i, n], (d, at_z(SIDES[n])))
-
-    def ret_start(i):
-        for n in range(2):
-            far_copy(i, n).wait_recv()
-            rout[i, n] = (near[i, n] + fhere[i, n].astype(F32)).astype(BF16)
-            ret_copy(i, n).start()
+        return remote(rout.at[i, n], rin.at[i, n], r_send.at[i, n], r_recv.at[i, n], (d, at_z(OFFSETS[n])))
 
     def g1_copy(i):
         return remote(g1send.at[i], g1recv.at[i], g1_send.at[i], g1_rsem.at[i], core_dev)
@@ -356,7 +348,7 @@
 
     def finish(i):
         total = own[i]
-        for n in range(2):
+        for n in range(4):
             ret_copy(i, n).wait_recv()
             total = total + rin[i, n].astype(F32)
         fin[i] = total.astype(BF16)
@@ -446,26 +438,19 @@
         w_pair = wbuf[pl.ds(doc_row, 2)].reshape(2 * HEAD_DIM, WIDTH)
         back(i, 0, w_pair)
         back(i, 1, w_pair)
-        for n in range(2):
-            first = 8 * n
-            fout[i, n] = acc[first:first + 2].astype(BF16)
-            far_copy(i, n).start()
-            near[i, n] = acc[2 + 4 * n:4 + 4 * n]
+        for n in range(4):
+            first = 4 + 2 * OFFSETS[n]
+            rout[i, n] = acc[first:first + 2].astype(BF16)
+            ret_copy(i, n).start()
         own[i] = acc[4:6]
         dq_own(i).start()
         dq_pair(i).start()
 
-        @pl.when(i > 0)
-        def _():
-            ret_start(i - 1)
-
         @pl.when(i > 1)
         def _():
             finish(i - 2)
 
     lax.fori_loop(0, STEPS + 1, step, 0)
-    ret_start(3)
-    finish(2)
 
     for i in range(STEPS):
         att_take(i).wait_recv()
@@ -475,6 +460,7 @@
         lob[:, piece] = dot(rows, wbuf[:, :, piece].reshape(WIDTH, 256)).astype(BF16)
     lo_copy = pltpu.make_async_copy(lob, lo_out, o_sem.at[0, 3])
     lo_copy.start()
+    finish(2)
 
     def g4_wait(o, total):
         g4_copy(o).wait_recv()
@@ -493,13 +479,21 @@
     def _():
         g3_copy(0, pair_dev).start()
         parts[0] = part[...]
-        g3_take(1).wait_recv()
-        g3_copy(0, pair_dev).wait_send()
 
     @pl.when(yh != y)
     def _():
         g3_copy(0, far_dev).start()
         g3_copy(1, (d_far, s)).start()
+
+    finish(3)
+
+    @pl.when(yh == y)
+    def _():
+        g3_take(1).wait_recv()
+        g3_copy(0, pair_dev).wait_send()
+
+    @pl.when(yh != y)
+    def _():
         g3_take(0).wait_recv()
         g3_take(1).wait_recv()
         g3_copy(0, far_dev).wait_send()
@@ -519,7 +513,6 @@
         return carry
 
     lax.fori_loop(1, Z, g5_start, 0)
-    finish(3)
 
     def g5_wait(o, carry):
         g5_take(o).wait_recv()
@@ -539,7 +532,7 @@
         for n in range(2):
             halo(i, n, False).wait_send()
             halo(i, n, True).wait_send()
-            far_copy(i, n).wait_send()
+        for n in range(4):
             ret_copy(i, n).wait_send()
         att_send(i).wait_send()
         dq_own(i).wait()
@@ -613,12 +606,9 @@
             vm((STEPS, 2) + block, BF16),
             vm((SLOTS, 2) + block, F32),
             vm((STEPS, 2, 2) + block, F32),
-            vm((STEPS, 2, 2, 2) + block, BF16),
-            vm((STEPS, 2, 2, 2) + block, BF16),
-            vm((STEPS, 2, 2, 2) + block, BF16),
-            vm((STEPS, 2, 2, 2) + block, BF16),
+            vm((STEPS, 4, 2, 2) + block, BF16),
+            vm((STEPS, 4, 2, 2) + block, BF16),
             vm((STEPS, 2, 2) + block, BF16),
-            vm((STEPS, 2, 2, 2) + block, F32),
             vm((STEPS, 2, HEAD_DIM, WIDTH), F32),
             vm((STEPS, HEAD_DIM, WIDTH), BF16),
             vm((STEPS, HEAD_DIM, WIDTH), BF16),
@@ -644,8 +634,7 @@
             dma((3,)), dma((3,)),
             dma((8,)), dma((8,)),
             dma((4,)), dma((4,)),
-            dma((STEPS, 2)), dma((STEPS, 2)),
-            dma((STEPS, 2)), dma((STEPS, 2)),
+            dma((STEPS, 4)), dma((STEPS, 4)),
             dma((STEPS,)), dma((STEPS,)),
             dma((STEPS,)), dma((STEPS,)),
             dma((STEPS, 2)), dma((STEPS, 2)),

time: 95.1 us -> 102 us (1.073)
  the two profiles are of different devices: /device:TPU:1 before, /device:TPU:6 now
where the time goes in v5:
time: 102 us
  Pallas kernels  101 us (99%)
    pallas_call x1, Pallas kernels, body(): pl.pallas_call(layer_kernel, out_shape=(rows_shape,) * 4 + (jax.ShapeDtyp...  99 us
    pallas_call x1, Pallas kernels, body(): pl.pallas_call(copy_kernel, out_shape=tuple((jax.ShapeDtypeStruct(a.shape...  2.09 us

profile of v5, /device:TPU:6, one launch (start us, length us, event | category | flops | bytes accessed | tf_op | source)
XLA Modules:
  0.0 101.7 jit_solution(2785595962196445663)
XLA Ops:
  0.6 99.0 %layer.1 = (bf16[128,1024]{1,0:T(8,128)(2,1)}, bf16[128,1024]{1,0:T(8,128)(2,1)}, bf16[128,1024]{1,0:T(8,128)(2,1)}, bf16[128,1024]{1,0:T(8,128)(2,1)}, f32[64,1024]{1,0:T(8,128)}) custom-call(s32[1,4]{1,0:T(1,128)} %lengths.1, s32[1,4]{1,0:T(1,128)} %upweight.1, bf16[128,1024]{1,0:T(8,128)(2,1)} %bitcast.8, bf16[128,1024]{1,0:T(8,128)(2,1)} %bitcast.9, ...), custom_call_target="tpu_custom_call" | custom-call | tf_op jit(solution)/shard_map/layer/pallas_call | solution.py:592
  99.6 2.1 %outputs.1 = (bf16[128,1024]{1,0:T(8,128)(2,1)}, bf16[128,1024]{1,0:T(8,128)(2,1)}, bf16[128,1024]{1,0:T(8,128)(2,1)}, bf16[128,1024]{1,0:T(8,128)(2,1)}, f32[64,1024]{1,0:T(8,128)}) custom-call(bf16[128,1024]{1,0:T(8,128)(2,1)} %get-tuple-element.15.refs_0_, bf16[128,1024]{1,0:T(8,128)(2,1)} %get-tuple-element.16.refs_1_, ...), custom_call_target="tpu_custom_call" | custom-call | tf_op jit(solution)/shard_map/outputs/pallas_call | solution.py:653

commit v6 on v3

--- a/solution.py
+++ b/solution.py
@@ -41,12 +41,12 @@
     lengths, upweight, q_in, k_in, v_in, ct_in, w_in,
     lo_out, dq_out, dk_out, dv_out, gw_out,
     qbuf, kv, ctb, gout, wbuf, bias, attbuf, attpair, dqb, acc, own, fout, fhere, rout, rin, fin,
-    near, gkeep, g1send, g1recv, g2send, g2recv, g4f, g4send, g4recv, part, parts, zag, gwo, lob,
+    near, gkeep, g1send, g1recv, g2send, g2recv, g2sum, g3send, g3recv, g4f, g4send, g4recv, zag, gwh, gwo, lob,
     s_scr, dp_scr, p_scr, ds_scr,
     l_sem, y_send, y_recv, ct_send, ct_recv, z_send, z_recv, zf_send, zf_recv, wx_send, wx_recv,
     wc_send, wc_recv, wy_send, wy_recv, r_send, r_recv, rf_send, rf_recv, a_send, a_recv,
     dq_send, dq_recv, f_send, f_recv, o_sem, g1_send, g1_rsem, g2_send, g2_rsem,
-    g3_send, g3_rsem, g4_send, g4_rsem, g5_send, g5_rsem,
+    g3_send, g3_rsem, g4_send, g4_rsem, g5_send, g5_rsem, g6_send, g6_rsem,
 ):
     d = lax.axis_index("doc")
     s = lax.axis_index("seq")
@@ -374,8 +374,16 @@
             remote(g2recv.at[i], g2recv.at[i], g2_send.at[i], g2_rsem.at[i], (at_x(1 + i), s)).wait_recv()
             head = head + g2recv[i].astype(F32)
         for j in range(8):
-            for half in range(2):
-                g4f[2 * j + half] = head[half * 32:half * 32 + 32, j * LANES:(j + 1) * LANES]
+            g2sum[j] = head[:, j * LANES:(j + 1) * LANES]
+        g3send[...] = g2sum[pl.ds((1 - yh) * 4, 4)].astype(BF16)
+        g3.start()
+
+    g3 = remote(g3send, g3recv, g3_send, g3_rsem, (d_far, s))
+
+    def z_pieces():
+        g3.wait_recv()
+        half_sum = g2sum[pl.ds(yh * 4, 4)] + g3recv[...].astype(F32)
+        g4f[...] = half_sum.reshape(Z, 16, LANES)
         g4send[...] = g4f[...].astype(BF16)
 
         def g4_start(o, carry):
@@ -437,6 +445,10 @@
         dq_own(i).start()
         dq_pair(i).start()
 
+        @pl.when(i == 3)
+        def _():
+            z_pieces()
+
         @pl.when(i > 0)
         def _():
             ret_start(i - 1)
@@ -464,32 +476,8 @@
         g4_copy(o).wait_recv()
         return total + g4recv[o].astype(F32)
 
-    part[...] = lax.fori_loop(1, Z, g4_wait, g4f[z])
-
-    def g3_copy(n, device):
-        slot = (yh + y) % 2
-        return remote(part, parts.at[slot], g3_send.at[n], g3_rsem.at[slot], device)
-
-    def g3_take(slot):
-        return remote(parts.at[slot], parts.at[slot], g3_send.at[0], g3_rsem.at[slot], pair_dev)
-
-    @pl.when(yh == y)
-    def _():
-        g3_copy(0, pair_dev).start()
-        parts[0] = part[...]
-        g3_take(1).wait_recv()
-        g3_copy(0, pair_dev).wait_send()
-
-    @pl.when(yh != y)
-    def _():
-        g3_copy(0, far_dev).start()
-        g3_copy(1, (d_far, s)).start()
-        g3_take(0).wait_recv()
-        g3_take(1).wait_recv()
-        g3_copy(0, far_dev).wait_send()
-        g3_copy(1, (d_far, s)).wait_send()
-
-    zag[z] = ((parts[0] + parts[1]) * (1.0 / math.sqrt(Z * 2 * ROWS * 16))).astype(BF16)
+    piece_sum = lax.fori_loop(1, Z, g4_wait, g4f[z])
+    zag[z] = (piece_sum * (1.0 / math.sqrt(Z * 2 * ROWS * 16))).astype(BF16)
 
     def g5_copy(o):
         return remote(zag.at[z], zag.at[z], g5_send.at[o], g5_rsem.at[o], (d, at_z(o)))
@@ -510,9 +498,32 @@
         return carry
 
     lax.fori_loop(1, Z, g5_wait, 0)
-    for j in range(8):
-        for half in range(2):
-            gwo[half * 32:half * 32 + 32, j * LANES:(j + 1) * LANES] = zag[2 * j + half].astype(F32)
+    def g6_copy(n, device):
+        return remote(zag, gwh.at[yh], g6_send.at[n], g6_rsem.at[yh], device)
+
+    def g6_take(part):
+        return remote(gwh.at[part], gwh.at[part], g6_send.at[0], g6_rsem.at[part], pair_dev)
+
+    @pl.when(yh == y)
+    def _():
+        g6_copy(0, pair_dev).start()
+        gwh[yh] = zag[...]
+        g6_take(1 - yh).wait_recv()
+        g6_copy(0, pair_dev).wait_send()
+
+    @pl.when(yh != y)
+    def _():
+        g6_copy(0, far_dev).start()
+        g6_copy(1, (d_far, s)).start()
+        g6_take(0).wait_recv()
+        g6_take(1).wait_recv()
+        g6_copy(0, far_dev).wait_send()
+        g6_copy(1, (d_far, s)).wait_send()
+
+    for part in range(2):
+        for j in range(4):
+            lanes = slice((part * 4 + j) * LANES, (part * 4 + j + 1) * LANES)
+            gwo[:, lanes] = gwh[part, 4 * j:4 * j + 4].reshape(HEAD_DIM, LANES).astype(F32)
     gw_copy = pltpu.make_async_copy(gwo, gw_out, o_sem.at[1, 3])
     gw_copy.start()
 
@@ -549,6 +560,8 @@
         remote(block, block, wc_send.at[o], wc_recv.at[o], core_dev).wait_send()
         block = w_block(1 - yh, o)
         remote(block, block, wc_send.at[4 + o], wc_recv.at[4 + o], core_dev).wait_send()
+
+    g3.wait_send()
 
     def drain_pieces(o, carry):
         g4_copy(o).wait_send()
@@ -608,12 +621,14 @@
             vm((STEPS, HEAD_DIM, WIDTH), BF16),
             vm((3, HEAD_DIM, WIDTH), BF16),
             vm((3, HEAD_DIM, WIDTH), BF16),
-            vm((Z, 32, LANES), F32),
-            vm((Z, 32, LANES), BF16),
-            vm((Z, 32, LANES), BF16),
-            vm((32, LANES), F32),
-            vm((2, 32, LANES), F32),
-            vm((Z, 32, LANES), BF16),
+            vm((8, HEAD_DIM, LANES), F32),
+            vm((4, HEAD_DIM, LANES), BF16),
+            vm((4, HEAD_DIM, LANES), BF16),
+            vm((Z, 16, LANES), F32),
+            vm((Z, 16, LANES), BF16),
+            vm((Z, 16, LANES), BF16),
+            vm((Z, 16, LANES), BF16),
+            vm((2, Z, 16, LANES), BF16),
             vm((HEAD_DIM, WIDTH), F32),
             vm((ROWS, WIDTH), BF16),
             vm((2, SPAN * ROWS, 2 * ROWS), F32),
@@ -636,9 +651,10 @@
             dma((STEPS, 4)),
             dma((STEPS,)), dma((STEPS,)),
             dma((3,)), dma((3,)),
-            dma((2,)), dma((2,)),
+            dma, dma,
             dma((Z,)), dma((Z,)),
             dma((Z,)), dma((Z,)),
+            dma((2,)), dma((2,)),
         ],
         compiler_params=pltpu.CompilerParams(
             collective_id=0, has_side_effects=True, vmem_limit_bytes=56 * 2**20

time: 93.6 us -> 90.1 us (0.963)
  Pallas kernels: 92.8 us -> 88.9 us
    pallas_call x1, Pallas kernels: 90.7 us -> 86.8 us  [body(): pl.pallas_call(layer_kernel, out_shape=(rows_shape,) * 4 + (jax.ShapeDtyp...]
where the time goes in v6:
time: 90.1 us; the launch traced here: 89.5 us
  Pallas kernels  88.9 us (99%)
    pallas_call x1, Pallas kernels, body(): pl.pallas_call(layer_kernel, out_shape=(rows_shape,) * 4 + (jax.ShapeDtyp...  86.8 us
    pallas_call x1, Pallas kernels, body(): pl.pallas_call(copy_kernel, out_shape=tuple((jax.ShapeDtypeStruct(a.shape...  2.09 us

profile of v6, /device:TPU:6, one launch (start us, length us, event | category | flops | bytes accessed | tf_op | source)
XLA Modules:
  0.0 89.5 jit_solution(5162916288027787820)
XLA Ops:
  0.6 86.8 %layer.1 = (bf16[128,1024]{1,0:T(8,128)(2,1)}, bf16[128,1024]{1,0:T(8,128)(2,1)}, bf16[128,1024]{1,0:T(8,128)(2,1)}, bf16[128,1024]{1,0:T(8,128)(2,1)}, f32[64,1024]{1,0:T(8,128)}) custom-call(s32[1,4]{1,0:T(1,128)} %lengths.1, s32[1,4]{1,0:T(1,128)} %upweight.1, bf16[128,1024]{1,0:T(8,128)(2,1)} %bitcast.8, bf16[128,1024]{1,0:T(8,128)(2,1)} %bitcast.9, ...), custom_call_target="tpu_custom_call" | custom-call | tf_op jit(solution)/shard_map/layer/pallas_call | solution.py:596
  87.4 2.1 %outputs.1 = (bf16[128,1024]{1,0:T(8,128)(2,1)}, bf16[128,1024]{1,0:T(8,128)(2,1)}, bf16[128,1024]{1,0:T(8,128)(2,1)}, bf16[128,1024]{1,0:T(8,128)(2,1)}, f32[64,1024]{1,0:T(8,128)}) custom-call(bf16[128,1024]{1,0:T(8,128)(2,1)} %get-tuple-element.15.refs_0_, bf16[128,1024]{1,0:T(8,128)(2,1)} %get-tuple-element.16.refs_1_, ...), custom_call_target="tpu_custom_call" | custom-call | tf_op jit(solution)/shard_map/outputs/pallas_call | solution.py:664

commit v7 on v6

--- a/solution.py
+++ b/solution.py
@@ -72,18 +72,6 @@
     core_dev = (d_core, s)
     far_dev = (d_far, s_pair)
 
-    barrier = pltpu.get_barrier_semaphore()
-    partners = [pair_dev, core_dev, far_dev, (d_far, s)] + [(at_x(o), s) for o in (1, 2, 3)]
-    for device in partners:
-        pl.semaphore_signal(barrier, inc=1, device_id=device, device_id_type=MESH)
-
-    def greet(o, carry):
-        pl.semaphore_signal(barrier, inc=1, device_id=(d, at_z(o)), device_id_type=MESH)
-        return carry
-
-    lax.fori_loop(1, Z, greet, 0)
-    pl.semaphore_wait(barrier, len(partners) + Z - 1)
-
     def own_kv(i):
         mine = cols(y, i)
         return [
@@ -94,6 +82,28 @@
     def own_q(i):
         return pltpu.make_async_copy(q_in.at[:, cols(y, i)], qbuf.at[i, y], l_sem.at[i, 2])
 
+    own_ct = pltpu.make_async_copy(ct_in, ctb.at[y], l_sem.at[0, 3])
+    own_w = pltpu.make_async_copy(w_in, wbuf.at[d], l_sem.at[1, 3])
+    for i in range(STEPS):
+        for copy in own_kv(i):
+            copy.start()
+    own_w.start()
+    for i in range(STEPS):
+        own_q(i).start()
+    own_ct.start()
+
+    barrier = pltpu.get_barrier_semaphore()
+    partners = [pair_dev, core_dev, far_dev, (d_far, s)] + [(at_x(o), s) for o in (1, 2, 3)]
+    for device in partners:
+        pl.semaphore_signal(barrier, inc=1, device_id=device, device_id_type=MESH)
+
+    def greet(o, carry):
+        pl.semaphore_signal(barrier, inc=1, device_id=(d, at_z(o)), device_id_type=MESH)
+        return carry
+
+    lax.fori_loop(1, Z, greet, 0)
+    pl.semaphore_wait(barrier, len(partners) + Z - 1)
+
     def pair_kv(i):
         theirs = cols(1 - y, i)
         return [
@@ -114,48 +124,58 @@
         here = qbuf.at[i, 1 - y]
         return remote(here, here, y_send.at[i, 2], y_recv.at[i, 2], pair_dev)
 
-    def halo(i, n, far, arrival=False):
+    def near_copy(i, n, part, arrival=False):
         o = SIDES[n]
-        to = 4 - 2 * o * (2 if far else 1)
-        here = to if arrival else (4 - 2 * o if far else 4)
-        send, recv = (zf_send, zf_recv) if far else (z_send, z_recv)
+        block = 4 + y if part == 0 else 5 - y
+        to = block - 2 * o
+        here = to if arrival else block
         return remote(
-            kv.at[i, pl.ds(here, 2)], kv.at[i, pl.ds(to, 2)], send.at[i, n], recv.at[i, n], (d, at_z(o))
+            kv.at[i, here], kv.at[i, to], z_send.at[i, n, part], z_recv.at[i, n, part], (d, at_z(o))
         )
 
-    own_ct = pltpu.make_async_copy(ct_in, ctb.at[y], l_sem.at[0, 3])
-    own_w = pltpu.make_async_copy(w_in, wbuf.at[d], l_sem.at[1, 3])
+    def halo(i, n, arrival=False):
+        o = SIDES[n]
+        to = 4 - 4 * o
+        here = to if arrival else 4 - 2 * o
+        return remote(
+            kv.at[i, pl.ds(here, 2)], kv.at[i, pl.ds(to, 2)], zf_send.at[i, n], zf_recv.at[i, n], (d, at_z(o))
+        )
+
     send_ct = remote(ct_in, ctb.at[y], ct_send, ct_recv, pair_dev)
     take_ct = remote(ctb.at[1 - y], ctb.at[1 - y], ct_send, ct_recv, pair_dev)
 
     def start_kv(i):
-        for copy in own_kv(i) + pair_kv(i):
+        for copy in pair_kv(i):
             copy.start()
 
     def start_q(i):
-        own_q(i).start()
         pair_q(i).start()
 
-    def start_near(i):
+    def own_near(i):
         for copy in own_kv(i):
             copy.wait()
+        for n in range(2):
+            near_copy(i, n, 0).start()
+
+    def start_near(i):
         for copy in take_kv(i):
             copy.wait_recv()
         for n in range(2):
-            halo(i, n, False).start()
+            near_copy(i, n, 1).start()
 
     def forward(i):
         for n in range(2):
-            halo(i, n, False, True).wait_recv()
-            halo(i, n, True).start()
+            for part in range(2):
+                near_copy(i, n, part, True).wait_recv()
+            halo(i, n).start()
 
     start_kv(0)
     start_kv(1)
     start_q(0)
-    own_w.start()
     for o in (1, 2, 3):
         remote(w_in, wbuf.at[d], wx_send.at[o - 1], wx_recv.at[o - 1], (at_x(o), s)).start()
-    own_ct.start()
+    own_near(0)
+    own_near(1)
     start_near(0)
     start_kv(2)
     start_q(1)
@@ -205,6 +225,7 @@
         remote(block, block, wc_send.at[o], wc_recv.at[o], core_dev).start()
 
     forward(0)
+    own_near(2)
     start_near(2)
 
     def grad_out_rows():
@@ -399,6 +420,7 @@
 
         @pl.when(i == 0)
         def _():
+            own_near(3)
             start_near(3)
 
         @pl.when(i > 0)
@@ -408,7 +430,7 @@
         own_q(i).wait()
         take_q(i).wait_recv()
         for n in range(2):
-            halo(i, n, True, True).wait_recv()
+            halo(i, n, True).wait_recv()
         mixed = [ahead(i, yp) for yp in range(2)]
         att_send(i).start()
         attbuf[y * 4 + pair_of(i)] = attpair[i, y]
@@ -532,8 +554,9 @@
             copy.wait_send()
         pair_q(i).wait_send()
         for n in range(2):
-            halo(i, n, False).wait_send()
-            halo(i, n, True).wait_send()
+            near_copy(i, n, 0).wait_send()
+            near_copy(i, n, 1).wait_send()
+            halo(i, n).wait_send()
             far_copy(i, n).wait_send()
             ret_copy(i, n).wait_send()
         att_send(i).wait_send()
@@ -638,7 +661,7 @@
             dma((STEPS, 4)),
             dma((STEPS, 3)), dma((STEPS, 3)),
             dma, dma,
-            dma((STEPS, 2)), dma((STEPS, 2)),
+            dma((STEPS, 2, 2)), dma((STEPS, 2, 2)),
             dma((STEPS, 2)), dma((STEPS, 2)),
             dma((3,)), dma((3,)),
             dma((8,)), dma((8,)),

time: 90.1 us -> 89.2 us (0.990)
  no operation moved by 1% of the time
where the time goes in v7:
time: 89.2 us; the launch traced here: 88.6 us
  Pallas kernels  88 us (99%)
    pallas_call x1, Pallas kernels, body(): pl.pallas_call(layer_kernel, out_shape=(rows_shape,) * 4 + (jax.ShapeDtyp...  85.9 us
    pallas_call x1, Pallas kernels, body(): pl.pallas_call(copy_kernel, out_shape=tuple((jax.ShapeDtypeStruct(a.shape...  2.09 us

profile of v7, /device:TPU:6, one launch (start us, length us, event | category | flops | bytes accessed | tf_op | source)
XLA Modules:
  0.0 88.6 jit_solution(13252847502309968195)
XLA Ops:
  0.6 85.9 %layer.1 = (bf16[128,1024]{1,0:T(8,128)(2,1)}, bf16[128,1024]{1,0:T(8,128)(2,1)}, bf16[128,1024]{1,0:T(8,128)(2,1)}, bf16[128,1024]{1,0:T(8,128)(2,1)}, f32[64,1024]{1,0:T(8,128)}) custom-call(s32[1,4]{1,0:T(1,128)} %lengths.1, s32[1,4]{1,0:T(1,128)} %upweight.1, bf16[128,1024]{1,0:T(8,128)(2,1)} %bitcast.8, bf16[128,1024]{1,0:T(8,128)(2,1)} %bitcast.9, ...), custom_call_target="tpu_custom_call" | custom-call | tf_op jit(solution)/shard_map/layer/pallas_call | solution.py:619
  86.5 2.1 %outputs.1 = (bf16[128,1024]{1,0:T(8,128)(2,1)}, bf16[128,1024]{1,0:T(8,128)(2,1)}, bf16[128,1024]{1,0:T(8,128)(2,1)}, bf16[128,1024]{1,0:T(8,128)(2,1)}, f32[64,1024]{1,0:T(8,128)}) custom-call(bf16[128,1024]{1,0:T(8,128)(2,1)} %get-tuple-element.15.refs_0_, bf16[128,1024]{1,0:T(8,128)(2,1)} %get-tuple-element.16.refs_1_, ...), custom_call_target="tpu_custom_call" | custom-call | tf_op jit(solution)/shard_map/outputs/pallas_call | solution.py:687

commit v8 on v7

--- a/solution.py
+++ b/solution.py
@@ -482,8 +482,6 @@
         return carry
 
     lax.fori_loop(0, STEPS, step, 0)
-    ret_start(3)
-    finish(2)
 
     for i in range(STEPS):
         att_take(i).wait_recv()
@@ -493,6 +491,8 @@
         lob[:, piece] = dot(rows, wbuf[:, :, piece].reshape(WIDTH, 256)).astype(BF16)
     lo_copy = pltpu.make_async_copy(lob, lo_out, o_sem.at[0, 3])
     lo_copy.start()
+    ret_start(3)
+    finish(2)
 
     def g4_wait(o, total):
         g4_copy(o).wait_recv()

time: 89.2 us -> 89.1 us (level)
  no operation moved by 1% of the time
where the time goes in v8:
time: 89.1 us; the launch traced here: 88.2 us
  Pallas kernels  87.5 us (98%)
    pallas_call x1, Pallas kernels, body(): pl.pallas_call(layer_kernel, out_shape=(rows_shape,) * 4 + (jax.ShapeDtyp...  85.4 us
    pallas_call x1, Pallas kernels, body(): pl.pallas_call(copy_kernel, out_shape=tuple((jax.ShapeDtypeStruct(a.shape...  2.09 us

profile of v8, /device:TPU:6, one launch (start us, length us, event | category | flops | bytes accessed | tf_op | source)
XLA Modules:
  0.0 88.2 jit_solution(18208703836492390828)
XLA Ops:
  0.6 85.4 %layer.1 = (bf16[128,1024]{1,0:T(8,128)(2,1)}, bf16[128,1024]{1,0:T(8,128)(2,1)}, bf16[128,1024]{1,0:T(8,128)(2,1)}, bf16[128,1024]{1,0:T(8,128)(2,1)}, f32[64,1024]{1,0:T(8,128)}) custom-call(s32[1,4]{1,0:T(1,128)} %lengths.1, s32[1,4]{1,0:T(1,128)} %upweight.1, bf16[128,1024]{1,0:T(8,128)(2,1)} %bitcast.8, bf16[128,1024]{1,0:T(8,128)(2,1)} %bitcast.9, ...), custom_call_target="tpu_custom_call" | custom-call | tf_op jit(solution)/shard_map/layer/pallas_call | solution.py:619
  86.1 2.1 %outputs.1 = (bf16[128,1024]{1,0:T(8,128)(2,1)}, bf16[128,1024]{1,0:T(8,128)(2,1)}, bf16[128,1024]{1,0:T(8,128)(2,1)}, bf16[128,1024]{1,0:T(8,128)(2,1)}, f32[64,1024]{1,0:T(8,128)}) custom-call(bf16[128,1024]{1,0:T(8,128)(2,1)} %get-tuple-element.15.refs_0_, bf16[128,1024]{1,0:T(8,128)(2,1)} %get-tuple-element.16.refs_1_, ...), custom_call_target="tpu_custom_call" | custom-call | tf_op jit(solution)/shard_map/outputs/pallas_call | solution.py:687
